TPU v7x, 32 devices: a whole 2x2x4 slice. The times are simulated.
32 devices in a mesh: dp: 8 (over z, y), tensor: 4 (over x, core).
Axes of the slice: x: 2, y: 2, z: 4, core: 2. Of those that a mesh axis runs over, the one named last changes fastest.
Arguments:
- tokens: bfloat16 [5120, 1536], P(('dp', 'tensor')), may hold values from -6 to 6
- cotangent: bfloat16 [5120, 1536], P(('dp', 'tensor')), may hold values from -6 to 6
- master: float32 [4, 8, 2482320], P('tensor', 'dp'), may hold values from -4.2 to 4.2
- first_moment: float32 [4, 8, 2482320], P('tensor', 'dp'), may hold values from -108 to 108
- second_moment: float32 [4, 8, 2482320], P('tensor', 'dp'), may hold values from 100 to 1000
- gain_master: float32 [6272], P(('dp', 'tensor')), may hold values from 0.28 to 2.4
- gain_first: float32 [6272], P(('dp', 'tensor')), may hold values from -108 to 108
- gain_second: float32 [6272], P(('dp', 'tensor')), may hold values from 1000 to 100000
Outputs:
- outputs: bfloat16 [5120, 1536], P(('dp', 'tensor'))
- input_grad: float32 [5120, 1536], P(('dp', 'tensor'))
- weight_grad: float32 [4, 8, 2482320], P('tensor', 'dp')
- new_master: float32 [4, 8, 2482320], P('tensor', 'dp')
- new_first: float32 [4, 8, 2482320], P('tensor', 'dp')
- new_second: float32 [4, 8, 2482320], P('tensor', 'dp')
- new_copy: bfloat16 [4, 8, 2482320], P('tensor', 'dp')
- gain_grad: float32 [6272], P(('dp', 'tensor'))
- new_gain_master: float32 [6272], P(('dp', 'tensor'))
- new_gain_first: float32 [6272], P(('dp', 'tensor'))
- new_gain_second: float32 [6272], P(('dp', 'tensor'))
- norms: float32 [2, 19], replicated
All inputs are finite; a program needn't handle non-finite values.
Results may differ from a plain program's by a relative error of at most 0.028.
The roundings to bfloat16 on the way count: a program that leaves them out, or rounds other values in their place, can miss the bound.
Values may be sent and summed in bfloat16 or wider, within the bound.
No kernel may reach another device: no remote copies, remote signals or barrier semaphores. Data moves between devices by JAX's collectives and lax.ppermute only.
A program may use at most 448 MiB of HBM per device.

v0:
```python
import math

import jax
import jax.numpy as jnp
import numpy as np
from jax import lax
from jax.sharding import PartitionSpec as P

MODEL_DIM = 1536
FEED_HIDDEN = 6912
QUERY_HEADS = 24
KEY_VALUE_HEADS = 8
HEAD_DIM = 64


NORM_EPS = 1e-05
ROPE_BASE = 1000000.0
BETA_FIRST = 0.9
BETA_SECOND = 0.99
ADAM_EPS = 1e-06
DECAY = 0.01
LEARN_RATE = 0.25
TRUST_EPS = 1e-06
MASK_FILL = -1e30


def weight_layout(model_width, conv_width, hidden_width, query_width, key_value_width):
    feed_shapes = [
        (model_width, hidden_width),
        (model_width, hidden_width),
        (hidden_width, model_width),
    ]
    return [
        [(model_width, 3, conv_width), (3, conv_width), (conv_width, model_width)],
        feed_shapes,
        [
            (model_width, query_width),
            (model_width, key_value_width),
            (model_width, key_value_width),
            (query_width, model_width),
        ],
        feed_shapes,
    ]


def rms_norm(values, gain_vec):
    return (
        values * lax.rsqrt(jnp.mean(values * values, axis=-1, keepdims=True) + NORM_EPS) * gain_vec
    )


def rope_tables(sequence_length):
    positions = jnp.arange(sequence_length, dtype=jnp.float32)
    inv_freq = ROPE_BASE ** (-jnp.arange(0, HEAD_DIM, 2, dtype=jnp.float32) / HEAD_DIM)
    angles = positions[:, None] * inv_freq[None, :]
    return (jnp.cos(angles)[:, None, :], jnp.sin(angles)[:, None, :])


def rotate(values, cosines, sines):
    half_dim = values.shape[-1] // 2
    first_half = values[..., :half_dim]
    second_half = values[..., half_dim:]
    return jnp.concatenate(
        [first_half * cosines - second_half * sines, second_half * cosines + first_half * sines],
        axis=-1,
    )


def head_prep(raw_rows, gain_vec, cosines, sines):
    sequence_length = raw_rows.shape[0]
    return rotate(
        rms_norm(raw_rows.reshape(sequence_length, -1, HEAD_DIM), gain_vec), cosines, sines
    )


def gated_unit(gate_vals, up_vals):
    return jax.nn.silu(gate_vals) * up_vals


def adam_terms(weight, grad_vals, first_old, second_old):
    first_new = BETA_FIRST * first_old + (1.0 - BETA_FIRST) * grad_vals
    second_new = BETA_SECOND * second_old + (1.0 - BETA_SECOND) * grad_vals * grad_vals
    update = first_new / (jnp.sqrt(second_new) + ADAM_EPS) + DECAY * weight
    return (first_new, second_new, update)


def dot_rows(lhs_rows, rhs_matrix):
    return jnp.dot(lhs_rows, rhs_matrix, preferred_element_type=jnp.float32)


def dot_first(lhs_rows, rhs_rows):
    return lax.dot_general(
        lhs_rows, rhs_rows, (((0,), (0,)), ((), ())), preferred_element_type=jnp.float32
    )


def dot_last(lhs_rows, rhs_matrix):
    return lax.dot_general(
        lhs_rows, rhs_matrix, (((1,), (1,)), ((), ())), preferred_element_type=jnp.float32
    )


def norm_back(values, gain_vec, grad_out):
    primal_out, pullback = jax.vjp(rms_norm, values, gain_vec)
    return pullback(grad_out)


def spread_rows(values):
    return lax.all_gather(values, "tensor", axis=0, tiled=True)


def spread_grads(values):
    return lax.all_gather(values, "tensor", axis=0, tiled=True)


def sum_branch(lhs_rows, rhs_matrix):
    return lax.psum_scatter(
        dot_rows(lhs_rows, rhs_matrix), "tensor", scatter_dimension=0, tiled=True
    )


def sum_input_grads(grad_pairs):
    running = None
    for grad_block, weight in grad_pairs:
        product_part = dot_last(grad_block, weight)
        running = product_part if running is None else running + product_part
    return lax.psum_scatter(running, "tensor", scatter_dimension=0, tiled=True)


def fetch_segment(shard_part, shapes, dp_count):
    gathered = lax.all_gather(
        shard_part.astype(jnp.bfloat16).reshape(1, -1), "dp", axis=0, tiled=True
    )
    result = []
    offset = 0
    for mat_shape in shapes:
        span_dev = math.prod(mat_shape) // dp_count
        result.append(gathered[:, offset : offset + span_dev].reshape(mat_shape))
        offset += span_dev
    return result


def whole_grad(entry):
    if entry[0] == "product":
        return dot_first(entry[1], entry[2]).reshape(entry[3])
    return entry[1]


def settle(grad_entries, dp_count):
    packed = jnp.concatenate(
        [whole_grad(entry).reshape(dp_count, -1) for entry in grad_entries], axis=1
    ).reshape(-1)
    return packed


def causal_mask(sequence_length):
    return jnp.arange(sequence_length)[:, None] >= jnp.arange(sequence_length)[None, :]


def score_block(query_b, key_b, causal):
    scores = jnp.einsum(
        "snge,tne->ngst", query_b, key_b, preferred_element_type=jnp.float32
    ) * HEAD_DIM ** (-0.5)
    return jnp.where(causal, scores, MASK_FILL)


def mixer_forward(residual, gain_vec, weights):
    w_in, kernel, w_out = weights
    conv_width = w_in.shape[2]
    normed_rows = spread_rows(rms_norm(residual, gain_vec).astype(jnp.bfloat16))
    projected = dot_rows(normed_rows, w_in.reshape(w_in.shape[0], -1)).reshape(-1, 3, conv_width)
    gate_b = projected[:, 0]
    gate_c = projected[:, 1]
    values = projected[:, 2]
    product = gate_b * values
    kernel_vals = kernel.astype(jnp.float32)
    padded = jnp.pad(product, ((2, 0), (0, 0)))
    conv_mixed = (
        kernel_vals[0] * padded[:-2] + kernel_vals[1] * padded[1:-1] + kernel_vals[2] * padded[2:]
    )
    conv_out = (gate_c * conv_mixed).astype(jnp.bfloat16)
    kept_vals = (normed_rows, gate_b, gate_c, values, padded, conv_mixed, conv_out)
    return (residual + sum_branch(conv_out, w_out), kept_vals)


def mixer_backward(grad_out, residual, gain_vec, weights, kept_vals):
    w_in, kernel, w_out = weights
    normed_rows, gate_b, gate_c, values, padded, conv_mixed, conv_out = kept_vals
    kernel_vals = kernel.astype(jnp.float32)
    grad_rows = spread_grads(grad_out.astype(jnp.bfloat16))
    d_conv = dot_last(grad_rows, w_out)
    d_gate_c = d_conv * conv_mixed
    d_mixed = d_conv * gate_c
    padded_grad = jnp.pad(d_mixed, ((0, 2), (0, 0)))
    d_product = (
        kernel_vals[0] * padded_grad[2:]
        + kernel_vals[1] * padded_grad[1:-1]
        + kernel_vals[2] * padded_grad[:-2]
    )
    d_kernel = jnp.stack(
        [
            jnp.sum(d_mixed * padded[:-2], axis=0),
            jnp.sum(d_mixed * padded[1:-1], axis=0),
            jnp.sum(d_mixed * padded[2:], axis=0),
        ]
    )
    d_gate_b = d_product * values
    d_values = d_product * gate_b
    d_proj = (
        jnp.stack([d_gate_b, d_gate_c, d_values], axis=1)
        .reshape(d_mixed.shape[0], -1)
        .astype(jnp.bfloat16)
    )
    w_flat = w_in.reshape(w_in.shape[0], -1)
    d_normed = sum_input_grads(((d_proj, w_flat),))
    d_resid, d_gain = norm_back(residual, gain_vec, d_normed)
    entries = [
        ("product", normed_rows, d_proj, w_in.shape),
        ("whole", d_kernel),
        ("product", conv_out, grad_rows, w_out.shape),
    ]
    return (grad_out + d_resid, d_gain, entries)


def ffn_forward(residual, gain_vec, weights):
    w_gate, w_up, w_down = weights
    normed_rows = spread_rows(rms_norm(residual, gain_vec).astype(jnp.bfloat16))
    gate_vals = dot_rows(normed_rows, w_gate)
    up_vals = dot_rows(normed_rows, w_up)
    hidden = gated_unit(gate_vals, up_vals).astype(jnp.bfloat16)
    return (residual + sum_branch(hidden, w_down), (normed_rows, gate_vals, up_vals, hidden))


def ffn_backward(grad_out, residual, gain_vec, weights, kept_vals):
    w_gate, w_up, w_down = weights
    normed_rows, gate_vals, up_vals, hidden = kept_vals
    grad_rows = spread_grads(grad_out.astype(jnp.bfloat16))
    d_hidden = dot_last(grad_rows, w_down)
    primal_out, pullback = jax.vjp(gated_unit, gate_vals, up_vals)
    d_gate, d_up = pullback(d_hidden)
    d_gate = d_gate.astype(jnp.bfloat16)
    d_up = d_up.astype(jnp.bfloat16)
    d_normed = sum_input_grads(((d_gate, w_gate), (d_up, w_up)))
    d_resid, d_gain = norm_back(residual, gain_vec, d_normed)
    entries = [
        ("product", normed_rows, d_gate, w_gate.shape),
        ("product", normed_rows, d_up, w_up.shape),
        ("product", hidden, grad_rows, w_down.shape),
    ]
    return (grad_out + d_resid, d_gain, entries)


def attention_forward(residual, gain_vec, gain_query, gain_key, weights, tables):
    w_query, key_matrix, value_matrix, w_attn = weights
    cosines, sines = tables
    normed_rows = spread_rows(rms_norm(residual, gain_vec).astype(jnp.bfloat16))
    seq_len = normed_rows.shape[0]
    q_heads = w_query.shape[1] // HEAD_DIM
    kv_heads = key_matrix.shape[1] // HEAD_DIM
    query_raw = dot_rows(normed_rows, w_query)
    key_raw = dot_rows(normed_rows, key_matrix)
    value_b = (
        dot_rows(normed_rows, value_matrix)
        .astype(jnp.bfloat16)
        .reshape(seq_len, kv_heads, HEAD_DIM)
    )
    query_b = (
        head_prep(query_raw, gain_query, cosines, sines)
        .astype(jnp.bfloat16)
        .reshape(seq_len, kv_heads, q_heads // kv_heads, HEAD_DIM)
    )
    key_b = head_prep(key_raw, gain_key, cosines, sines).astype(jnp.bfloat16)
    causal = causal_mask(seq_len)
    scores = score_block(query_b, key_b, causal)
    top_score = jnp.max(scores, axis=-1, keepdims=True)
    exp_scores = jnp.exp(scores - top_score)
    exp_total = jnp.sum(exp_scores, axis=-1, keepdims=True)
    log_sum = top_score + jnp.log(exp_total)
    soft_probs = (exp_scores / exp_total).astype(jnp.bfloat16)
    attended = jnp.einsum("ngst,tne->snge", soft_probs, value_b, preferred_element_type=jnp.float32)
    attended = attended.reshape(seq_len, -1).astype(jnp.bfloat16)
    kept_vals = (normed_rows, query_raw, key_raw, query_b, key_b, value_b, log_sum, attended)
    return (residual + sum_branch(attended, w_attn), kept_vals)


def attention_backward(
    grad_out, residual, gain_vec, gain_query, gain_key, weights, tables, kept_vals
):
    w_query, key_matrix, value_matrix, w_attn = weights
    cosines, sines = tables
    normed_rows, query_raw, key_raw, query_b, key_b, value_b, log_sum, attended = kept_vals
    seq_len = normed_rows.shape[0]
    grad_rows = spread_grads(grad_out.astype(jnp.bfloat16))
    d_attended = dot_last(grad_rows, w_attn).astype(jnp.bfloat16).reshape(query_b.shape)
    soft_probs = jnp.exp(score_block(query_b, key_b, causal_mask(seq_len)) - log_sum)
    d_probs = jnp.einsum("snge,tne->ngst", d_attended, value_b, preferred_element_type=jnp.float32)
    d_value = jnp.einsum(
        "ngst,snge->tne",
        soft_probs.astype(jnp.bfloat16),
        d_attended,
        preferred_element_type=jnp.float32,
    )
    row_dot = jnp.sum(soft_probs * d_probs, axis=-1, keepdims=True)
    d_scores = (soft_probs * (d_probs - row_dot)).astype(jnp.bfloat16)
    score_scale = HEAD_DIM ** (-0.5)
    d_query = (
        jnp.einsum("ngst,tne->snge", d_scores, key_b, preferred_element_type=jnp.float32)
        * score_scale
    )
    d_key = (
        jnp.einsum("ngst,snge->tne", d_scores, query_b, preferred_element_type=jnp.float32)
        * score_scale
    )
    primal_query, pull_query = jax.vjp(
        lambda raw_rows, gain_vals: head_prep(raw_rows, gain_vals, cosines, sines),
        query_raw,
        gain_query,
    )
    d_query_raw, d_gain_query = pull_query(d_query.reshape(seq_len, -1, HEAD_DIM))
    primal_key, pull_key = jax.vjp(
        lambda raw_rows, gain_vals: head_prep(raw_rows, gain_vals, cosines, sines),
        key_raw,
        gain_key,
    )
    d_key_raw, d_gain_key = pull_key(d_key)
    d_query_raw = d_query_raw.astype(jnp.bfloat16)
    d_key_raw = d_key_raw.astype(jnp.bfloat16)
    d_value_b = d_value.reshape(seq_len, -1).astype(jnp.bfloat16)
    d_normed = sum_input_grads(
        ((d_query_raw, w_query), (d_key_raw, key_matrix), (d_value_b, value_matrix))
    )
    d_resid, d_gain = norm_back(residual, gain_vec, d_normed)
    entries = [
        ("product", normed_rows, d_query_raw, w_query.shape),
        ("product", normed_rows, d_key_raw, key_matrix.shape),
        ("product", normed_rows, d_value_b, value_matrix.shape),
        ("product", attended, grad_rows, w_attn.shape),
    ]
    return (grad_out + d_resid, d_gain, d_gain_query, d_gain_key, entries)


def local(
    tokens, cotangent, master, first_moment, second_moment, gain_master, gain_first, gain_second
):
    dp_count = lax.axis_size("dp")
    tensor_shard_count = lax.axis_size("tensor")
    weight_segments = weight_layout(
        MODEL_DIM,
        MODEL_DIM // tensor_shard_count,
        FEED_HIDDEN // tensor_shard_count,
        QUERY_HEADS // tensor_shard_count * HEAD_DIM,
        KEY_VALUE_HEADS // tensor_shard_count * HEAD_DIM,
    )
    local_master = master.reshape(-1)
    weights = []
    mat_spans = []
    offset = 0
    for segment in weight_segments:
        seg_width = sum((math.prod(mat_shape) for mat_shape in segment)) // dp_count
        weights.append(fetch_segment(local_master[offset : offset + seg_width], segment, dp_count))
        mat_spans = mat_spans + [math.prod(mat_shape) // dp_count for mat_shape in segment]
        offset += seg_width
    gain_vector = lax.all_gather(gain_master, ("dp", "tensor"), axis=0, tiled=True)
    gain_one = gain_vector[0:MODEL_DIM]
    gain_two = gain_vector[MODEL_DIM : 2 * MODEL_DIM]
    gain_three = gain_vector[2 * MODEL_DIM : 3 * MODEL_DIM]
    gain_four = gain_vector[3 * MODEL_DIM : 4 * MODEL_DIM]
    gain_query = gain_vector[4 * MODEL_DIM : 4 * MODEL_DIM + HEAD_DIM]
    gain_key = gain_vector[4 * MODEL_DIM + HEAD_DIM : 4 * MODEL_DIM + 2 * HEAD_DIM]
    rows_dev = tokens.shape[0]
    tables = rope_tables(rows_dev * tensor_shard_count)
    resid_zero = tokens.astype(jnp.float32)
    resid_one, kept_mix = mixer_forward(resid_zero, gain_one, weights[0])
    resid_two, kept_ffn_one = ffn_forward(resid_one, gain_two, weights[1])
    resid_three, kept_attn = attention_forward(
        resid_two, gain_three, gain_query, gain_key, weights[2], tables
    )
    resid_four, kept_ffn_two = ffn_forward(resid_three, gain_four, weights[3])
    pending = [None, None, None, None]
    grad_four = cotangent.astype(jnp.float32)
    grad_three, d_gain_four, grads_ffn_two = ffn_backward(
        grad_four, resid_three, gain_four, weights[3], kept_ffn_two
    )
    pending[3] = settle(grads_ffn_two, dp_count)
    grad_two, d_gain_three, d_gain_query, d_gain_key, grads_attn = attention_backward(
        grad_three, resid_two, gain_three, gain_query, gain_key, weights[2], tables, kept_attn
    )
    pending[2] = settle(grads_attn, dp_count)
    grad_one, d_gain_two, grads_ffn_one = ffn_backward(
        grad_two, resid_one, gain_two, weights[1], kept_ffn_one
    )
    pending[1] = settle(grads_ffn_one, dp_count)
    grad_zero, d_gain_one, grads_mix = mixer_backward(
        grad_one, resid_zero, gain_one, weights[0], kept_mix
    )
    pending[0] = settle(grads_mix, dp_count)
    reduced = (
        lax.psum_scatter(pending[0], "dp", scatter_dimension=0, tiled=True),
        lax.psum_scatter(pending[1], "dp", scatter_dimension=0, tiled=True),
        lax.psum_scatter(pending[2], "dp", scatter_dimension=0, tiled=True),
        lax.psum_scatter(pending[3], "dp", scatter_dimension=0, tiled=True),
    )
    grad_local = jnp.concatenate([grad_part for grad_part in reduced])
    gain_partial = jnp.concatenate(
        [d_gain_one, d_gain_two, d_gain_three, d_gain_four, d_gain_query, d_gain_key]
    )
    gain_grad = lax.psum_scatter(gain_partial, ("dp", "tensor"), scatter_dimension=0, tiled=True)
    first_new, second_new, update = adam_terms(
        local_master, grad_local, first_moment.reshape(-1), second_moment.reshape(-1)
    )
    gain_first_new, gain_second_new, gain_update = adam_terms(
        gain_master, gain_grad, gain_first, gain_second
    )
    bounds = np.cumsum([0] + mat_spans)
    weight_sq = jnp.stack(
        [
            jnp.sum(local_master[bounds[number] : bounds[number + 1]] ** 2)
            for number in range(len(mat_spans))
        ]
    )
    update_sq = jnp.stack(
        [
            jnp.sum(update[bounds[number] : bounds[number + 1]] ** 2)
            for number in range(len(mat_spans))
        ]
    )
    gain_count = gain_master.shape[0]
    positions = lax.axis_index(("dp", "tensor")) * gain_count + jnp.arange(
        gain_count, dtype=jnp.int32
    )
    gain_edges = jnp.asarray(
        np.cumsum([0, MODEL_DIM, MODEL_DIM, MODEL_DIM, MODEL_DIM, HEAD_DIM, HEAD_DIM]), jnp.int32
    )
    member = (
        (positions[:, None] >= gain_edges[None, :-1]) & (positions[:, None] < gain_edges[None, 1:])
    ).astype(jnp.float32)
    gain_wsq = jnp.sum((gain_master * gain_master)[:, None] * member, axis=0)
    gain_usq = jnp.sum((gain_update * gain_update)[:, None] * member, axis=0)
    weight_total, update_total = lax.psum(
        (jnp.concatenate([weight_sq, gain_wsq]), jnp.concatenate([update_sq, gain_usq])),
        ("dp", "tensor"),
    )
    weight_norm = jnp.sqrt(weight_total)
    update_norm = jnp.sqrt(update_total)
    trust_ratio = weight_norm / (update_norm + TRUST_EPS)
    mat_count = len(mat_spans)
    mat_ratio = jnp.repeat(
        trust_ratio[:mat_count], np.array(mat_spans), total_repeat_length=local_master.shape[0]
    )
    gain_ratio = jnp.sum(member * trust_ratio[None, mat_count:], axis=1)
    new_master = local_master - LEARN_RATE * mat_ratio * update
    new_gain_master = gain_master - LEARN_RATE * gain_ratio * gain_update
    norms = jnp.stack([weight_norm, update_norm])
    return (
        resid_four.astype(jnp.bfloat16),
        grad_zero,
        grad_local.reshape(master.shape),
        new_master.reshape(master.shape),
        first_new.reshape(master.shape),
        second_new.reshape(master.shape),
        new_master.astype(jnp.bfloat16).reshape(master.shape),
        gain_grad,
        new_gain_master,
        gain_first_new,
        gain_second_new,
        norms,
    )


def solution(mesh):
    in_specs = (
        P(("dp", "tensor"), None),
        P(("dp", "tensor"), None),
        P("tensor", "dp", None),
        P("tensor", "dp", None),
        P("tensor", "dp", None),
        P(("dp", "tensor")),
        P(("dp", "tensor")),
        P(("dp", "tensor")),
    )
    out_specs = (
        P(("dp", "tensor"), None),
        P(("dp", "tensor"), None),
        P("tensor", "dp", None),
        P("tensor", "dp", None),
        P("tensor", "dp", None),
        P("tensor", "dp", None),
        P("tensor", "dp", None),
        P(("dp", "tensor")),
        P(("dp", "tensor")),
        P(("dp", "tensor")),
        P(("dp", "tensor")),
        P(),
    )
    return jax.shard_map(local, mesh=mesh, in_specs=in_specs, out_specs=out_specs, check_vma=False)
```

profile of v0, /device:TPU:0, one launch (start us, length us, event | category | flops | bytes accessed | tf_op | source)
XLA Modules:
  0.0 5392.4 jit_solution(7994552808349285148)
XLA Ops:
  7.2 115.7 %multiply_reduce_fusion = (f32[2482320]{0:T(1024)}, bf16[1,1,2482320]{2,1,0:T(2,128)(2,1)}) fusion(f32[1,1,2482320]{2,1,0:T(1,128)} %param.14), kind=kLoop, calls=%fused_computation.29 | loop fusion | flops 4964640 | bytes 24823200 | tf_op jit(solution)/shard_map/mul | solution.py:83
  127.0 46.4 all-reduce.11
  178.8 89.0 %all-gather.33.cloned.1.call-done = bf16[8,1,295056]{2,1,0:T(2,128)(2,1)} async-done(((bf16[1,1,295056]{2,1,0:T(2,128)(2,1)}), bf16[8,1,295056]{2,1,0:T(2,128)(2,1)}) %all-gather.33.cloned.1.call-update) | async-done | bytes 4720912 | tf_op jit(solution)/shard_map/all_gather | solution.py:131
  304.7 11.5 fusion.89
  319.6 72.0 %all-gather.37.cloned.1.call-done = bf16[8,1,196608]{2,1,0:T(2,128)(2,1)} async-done(((bf16[1,1,196608]{2,1,0:T(2,128)(2,1)}), bf16[8,1,196608]{2,1,0:T(2,128)(2,1)}) %all-gather.37.cloned.1.call-update) | async-done | bytes 3145744 | tf_op jit(solution)/shard_map/all_gather | solution.py:131
  399.5 36.1 reduce-scatter.9.cloned.1.call-done
  438.6 604.7 %all-gather.35.cloned.1.call-done = bf16[8,1,995328]{2,1,0:T(2,128)(2,1)} async-done(((bf16[1,1,995328]{2,1,0:T(2,128)(2,1)}), bf16[8,1,995328]{2,1,0:T(2,128)(2,1)}) %all-gather.35.cloned.1.call-update) | async-done | bytes 15925264 | tf_op jit(solution)/shard_map/all_gather | solution.py:131
  1043.4 14.7 copy.101
  1133.8 36.6 reduce-scatter.11.cloned.1.call-done
  1178.3 16.4 all-gather.21.cloned.1.call-done
  1212.6 42.4 reduce-scatter.13.cloned.1.call-done
  1259.5 602.6 %all-gather.39.cloned.1.call-done = bf16[8,1,995328]{2,1,0:T(2,128)(2,1)} async-done(((bf16[1,1,995328]{2,1,0:T(2,128)(2,1)}), bf16[8,1,995328]{2,1,0:T(2,128)(2,1)}) %all-gather.39.cloned.1.call-update) | async-done | bytes 15925264 | tf_op jit(solution)/shard_map/all_gather | solution.py:131
  1862.1 14.7 copy.100
  1907.1 10.0 reshape.698
  1940.7 13.2 multiply_convert_fusion.1
  1969.6 43.1 reduce-scatter.17.cloned.1.call-done
  2019.8 20.6 all-gather.27.cloned.1.call-done
  2051.5 10.6 fusion.8
  2089.8 33.7 reduce-scatter.19.cloned.1.call-done
  2125.6 43.9 reduce-scatter.15.cloned.1.call-done
  2173.1 21.7 all-gather.29.cloned.1.call-done
  2194.8 11.2 multiply_convert_fusion
  2231.4 10.5 reshape.716
  2250.7 13.3 reshape.781
  2282.8 13.4 reshape.783
  2306.2 26.9 maximum_bitcast_fusion.1
  2333.1 27.0 copy.95
  2394.1 10.5 fusion.112
  2404.6 10.1 reshape.707
  2423.8 13.3 reshape.777
  2455.6 13.3 reshape.779
  2478.7 26.8 maximum_bitcast_fusion
  2505.5 27.1 copy.93
  2586.6 12.9 reshape.704
  2613.2 19.4 multiply_reduce_fusion.3
  2632.8 112.2 %multiply_reduce_fusion.1 = (f32[2482320]{0:T(1024)}, f32[2482320]{0:T(1024)}) fusion(f32[1,1,2482320]{2,1,0:T(1,128)} %param.16, f32[1,1,2482320]{2,1,0:T(1,128)} %param.15), kind=kLoop, calls=%fused_computation.30 | loop fusion | flops 4964640 | bytes 39717120 | tf_op jit(solution)/shard_map/mul | solution.py:82
  2746.7 44.0 all-reduce.16
  2802.4 2111.0 %all-reduce.21.cloned.1.call-done = (f32[2360448]{0:T(1024)}, f32[7962624]{0:T(1024)}, f32[1572864]{0:T(1024)}, f32[7962624]{0:T(1024)}) async-done(((f32[2360448]{0:T(1024)}, f32[7962624]{0:T(1024)}, f32[1572864]{0:T(1024)}, f32[7962624]{0:T(1024)}), (f32[2360448]{0:T(1024)}, f32[7962624]{0:T(1024)}, f32[1572864]{0:T(1024)}, f32[7962624]{0:T(1024)})) %all-reduce.21.cloned.1.call-update) | async-done | bytes 79434256
  4924.9 79.6 %concatenate.83 = f32[2482320]{0:T(1024)} concatenate(f32[295056]{0:T(1024)S(1)} %dynamic-slice.7, f32[995328]{0:T(1024)} %dynamic-slice.9, f32[196608]{0:T(1024)S(1)} %dynamic-slice.11, f32[995328]{0:T(1024)} %dynamic-slice.13), dimensions={0} | concatenate | bytes 19858560 | tf_op jit(solution)/shard_map/concatenate | solution.py:403
  5004.4 38.6 reshape.718
  5043.0 11.5 fusion.4
  5074.9 39.7 all-reduce.17
  5115.4 19.9 dynamic-update-slice.4
  5135.3 68.9 %dynamic-update-slice.5 = f32[1,1,2482320]{2,1,0:T(1,128)} dynamic-update-slice(f32[1,1,2482320]{2,1,0:T(1,128)} %dynamic-update-slice.4, f32[1,1,995328]{2,1,0:T(1,128)} %bitcast.247, s32[]{} %constant.285, s32[]{} %constant.285, s32[]{} %constant.286) | dynamic-update-slice | bytes 7962628
  5204.2 14.8 dynamic-update-slice.6
  5219.1 69.0 %dynamic-update-slice.7 = f32[1,1,2482320]{2,1,0:T(1,128)} dynamic-update-slice(f32[1,1,2482320]{2,1,0:T(1,128)} %dynamic-update-slice.6, f32[1,1,995328]{2,1,0:T(1,128)} %bitcast.246, s32[]{} %constant.285, s32[]{} %constant.285, s32[]{} %constant.288) | dynamic-update-slice | bytes 7962628 | tf_op jit(solution)/shard_map/concatenate | solution.py:403
  5288.1 26.0 select_multiply_fusion
  5314.1 70.1 %fusion.78 = (bf16[1,1,2482320]{2,1,0:T(2,128)(2,1)}, f32[1,1,2482320]{2,1,0:T(1,128)}, f32[1,1,2482320]{2,1,0:T(1,128)}, f32[1,1,2482320]{2,1,0:T(1,128)}) fusion(f32[1,1,2482320]{2,1,0:T(1,128)} %param.14, f32[2482320]{0:T(1024)} %select_multiply_fusion, f32[1,1,2482320]{2,1,0:T(1,128)} %dynamic-update-slice.7, f32[1,1,2482320]{2,1,0:T(1,128)} %param.16, ...), kind=kLoop, calls=%fused_computation.229 | loop fusion | flops 34752480 | bytes 84398880 | tf_op jit(solution)/shard_map/convert_element_type | solution.py:461
  (481 shorter events, 533.7 us)
Async XLA Ops:
  7.2 119.6 %copy-start.103 = (f32[196]{0:T(256)S(1)}, f32[196]{0:T(256)}, u32[]{:S(2)}) copy-start(f32[196]{0:T(256)} %param.17) | copy-start | bytes 2356
  7.2 166.2 %copy-start.10 = (bf16[160,1536]{1,0:T(8,128)(2,1)S(1)}, bf16[160,1536]{1,0:T(8,128)(2,1)}, u32[]{:S(2)}) copy-start(bf16[160,1536]{1,0:T(8,128)(2,1)} %param.12) | copy-start | bytes 1474564
  7.2 260.7 %all-gather.33.cloned.1.call-start = ((), (), s32[]{:S(2)}) async-start(), calls=%async_computation.24 | async-start | bytes 10626048 | tf_op jit(solution)/shard_map/all_gather | solution.py:131
  126.7 165.8 %all-gather.17.cloned.1.call-start = ((), (), s32[]{:S(2)}) async-start(), calls=%async_computation.8 | async-start | bytes 2457600 | tf_op jit(solution)/shard_map/all_gather | solution.py:109
  173.4 99.9 %copy-start.63 = (f32[6272]{0:T(1024)}, f32[6272]{0:T(1024)S(1)}, u32[]{:S(2)}) copy-start(f32[6272]{0:T(1024)S(1)} %all-reduce.11) | copy-start | bytes 75268
  174.2 99.2 %copy-start.90 = (f32[160]{0:T(256)}, f32[160]{0:T(256)S(1)}, u32[]{:S(2)}) copy-start(f32[160]{0:T(256)S(1)} %fusion.70) | copy-start | bytes 1924
  174.8 98.6 %copy-start.64 = (f32[1536]{0:T(1024)}, f32[1536]{0:T(1024)S(1)}, u32[]{:S(2)}) copy-start(f32[1536]{0:T(1024)S(1)} %get-tuple-element.127) | copy-start | bytes 18436
  174.8 262.3 %copy-start.66 = (f32[1536]{0:T(1024)}, f32[1536]{0:T(1024)S(1)}, u32[]{:S(2)}) copy-start(f32[1536]{0:T(1024)S(1)} %get-tuple-element.126) | copy-start | bytes 18436
  175.8 215.8 %all-gather.37.cloned.1.call-start = ((), (), s32[]{:S(2)}) async-start(), calls=%async_computation.26 | async-start | bytes 7077888 | tf_op jit(solution)/shard_map/all_gather | solution.py:131
  178.6 257.0 %reduce-scatter.9.cloned.1.call-start = ((), (), s32[]{:S(2)}) async-start(), calls=%async_computation.9 | async-start | bytes 4915200 | tf_op jit(solution)/shard_map/reduce_scatter | solution.py:117
  304.6 738.7 %all-gather.35.cloned.1.call-start = ((), (), s32[]{:S(2)}) async-start(), calls=%async_computation.25 | async-start | bytes 35831808 | tf_op jit(solution)/shard_map/all_gather | solution.py:131
  316.2 789.2 %all-gather.19.cloned.1.call-start = ((), (), s32[]{:S(2)}) async-start(), calls=%async_computation.10 | async-start | bytes 2457600 | tf_op jit(solution)/shard_map/all_gather | solution.py:109
  319.6 116.1 %copy-start.11 = (bf16[160,1536]{1,0:T(8,128)(2,1)S(1)}, bf16[160,1536]{1,0:T(8,128)(2,1)}, u32[]{:S(2)}) copy-start(bf16[160,1536]{1,0:T(8,128)(2,1)} %param.12) | copy-start | bytes 1474564
  437.0 621.0 %copy-start.98 = (f32[160]{0:T(256)}, f32[160]{0:T(256)S(1)}, u32[]{:S(2)}) copy-start(f32[160]{0:T(256)S(1)} %get-tuple-element.92) | copy-start | bytes 1924
  437.0 733.3 %copy-start.5 = (f32[160,1536]{1,0:T(8,128)}, f32[160,1536]{1,0:T(8,128)S(1)}, u32[]{:S(2)}) copy-start(f32[160,1536]{1,0:T(8,128)S(1)} %get-tuple-element.93) | copy-start | bytes 2949124
  437.1 621.0 %copy-start.92 = (f32[160]{0:T(256)}, f32[160]{0:T(256)S(1)}, u32[]{:S(2)}) copy-start(f32[160]{0:T(256)S(1)} %fusion.71) | copy-start | bytes 1924
  438.2 732.2 %reduce-scatter.11.cloned.1.call-start = ((), (), s32[]{:S(2)}) async-start(), calls=%async_computation.11 | async-start | bytes 4915200 | tf_op jit(solution)/shard_map/reduce_scatter | solution.py:117
  1127.3 67.5 %all-gather.21.cloned.1.call-start = ((), (), s32[]{:S(2)}) async-start(), calls=%async_computation.12 | async-start | bytes 2457600 | tf_op jit(solution)/shard_map/all_gather | solution.py:109
  1172.8 82.2 %reduce-scatter.13.cloned.1.call-start = ((), (), s32[]{:S(2)}) async-start(), calls=%async_computation.13 | async-start | bytes 4915200 | tf_op jit(solution)/shard_map/reduce_scatter | solution.py:117
  1211.9 650.2 %all-gather.39.cloned.1.call-start = ((), (), s32[]{:S(2)}) async-start(), calls=%async_computation.27 | async-start | bytes 35831808 | tf_op jit(solution)/shard_map/all_gather | solution.py:131
  1212.5 711.8 %all-gather.23.cloned.1.call-start = ((), (), s32[]{:S(2)}) async-start(), calls=%async_computation.14 | async-start | bytes 2457600 | tf_op jit(solution)/shard_map/all_gather | solution.py:109
  1258.5 682.2 %all-gather.25.cloned.1.call-start = ((), (), s32[]{:S(2)}) async-start(), calls=%async_computation.16 | async-start | bytes 2457600 | tf_op jit(solution)/shard_map/all_gather | solution.py:113
  1259.0 753.7 %reduce-scatter.17.cloned.1.call-start = ((), (), s32[]{:S(2)}) async-start(), calls=%async_computation.17 | async-start | bytes 4915200 | tf_op jit(solution)/shard_map/reduce_scatter | solution.py:127
  1969.6 70.8 %all-gather.27.cloned.1.call-start = ((), (), s32[]{:S(2)}) async-start(), calls=%async_computation.18 | async-start | bytes 2457600 | tf_op jit(solution)/shard_map/all_gather | solution.py:113
  2018.4 105.1 %reduce-scatter.19.cloned.1.call-start = ((), (), s32[]{:S(2)}) async-start(), calls=%async_computation.19 | async-start | bytes 4915200 | tf_op jit(solution)/shard_map/reduce_scatter | solution.py:127
  2080.4 89.0 %reduce-scatter.15.cloned.1.call-start = ((), (), s32[]{:S(2)}) async-start(), calls=%async_computation.15 | async-start | bytes 4915200 | tf_op jit(solution)/shard_map/reduce_scatter | solution.py:117
  2089.7 79.7 %copy-start.27 = (bf16[160,1536]{1,0:T(8,128)(2,1)S(1)}, bf16[160,1536]{1,0:T(8,128)(2,1)}, u32[]{:S(2)}) copy-start(bf16[160,1536]{1,0:T(8,128)(2,1)} %param.13) | copy-start | bytes 1474564
  2089.7 79.7 %copy-start.79 = (f32[160]{0:T(256)S(1)}, f32[160]{0:T(256)}, u32[]{:S(2)}) copy-start(f32[160]{0:T(256)} %copy-done.78) | copy-start | bytes 1924
  2089.8 105.0 %all-gather.29.cloned.1.call-start = ((), (), s32[]{:S(2)}) async-start(), calls=%async_computation.20 | async-start | bytes 2457600 | tf_op jit(solution)/shard_map/all_gather | solution.py:113
  2172.8 216.6 %reduce-scatter.21.cloned.1.call-start = ((), (), s32[]{:S(2)}) async-start(), calls=%async_computation.21 | async-start | bytes 4915200 | tf_op jit(solution)/shard_map/reduce_scatter | solution.py:127
  2222.0 310.6 %all-gather.31.cloned.1.call-start = ((), (), s32[]{:S(2)}) async-start(), calls=%async_computation.22 | async-start | bytes 2457600 | tf_op jit(solution)/shard_map/all_gather | solution.py:113
  2394.1 350.9 %reduce-scatter.23.cloned.1.call-start = ((), (), s32[]{:S(2)}) async-start(), calls=%async_computation.23 | async-start | bytes 4915200 | tf_op jit(solution)/shard_map/reduce_scatter | solution.py:127
  2549.9 2363.4 %all-reduce.21.cloned.1.call-start = ((), (), s32[]{:S(2)}) async-start(), calls=%async_computation.28 | async-start | bytes 158875648
  2632.7 112.3 %copy-start.12 = (bf16[160,1536]{1,0:T(8,128)(2,1)S(1)}, bf16[160,1536]{1,0:T(8,128)(2,1)}, u32[]{:S(2)}) copy-start(bf16[160,1536]{1,0:T(8,128)(2,1)} %param.12) | copy-start | bytes 1474564
  2632.7 112.3 %copy-start.65 = (f32[1536]{0:T(1024)S(1)}, f32[1536]{0:T(1024)}, u32[]{:S(2)}) copy-start(f32[1536]{0:T(1024)} %copy-done.64) | copy-start | bytes 18436
  2632.7 112.3 %copy-start.91 = (f32[160]{0:T(256)S(1)}, f32[160]{0:T(256)}, u32[]{:S(2)}) copy-start(f32[160]{0:T(256)} %copy-done.90) | copy-start | bytes 1924
  2632.7 113.9 %copy-start.75 = (f32[1536]{0:T(1024)S(1)}, f32[1536]{0:T(1024)}, u32[]{:S(2)}) copy-start(f32[1536]{0:T(1024)} %get-tuple-element.48) | copy-start | bytes 18436
  2632.7 113.9 %copy-start.76 = (f32[1536]{0:T(1024)S(1)}, f32[1536]{0:T(1024)}, u32[]{:S(2)}) copy-start(f32[1536]{0:T(1024)} %get-tuple-element.50) | copy-start | bytes 18436
  2632.7 113.9 %copy-start.77 = (f32[1536]{0:T(1024)S(1)}, f32[1536]{0:T(1024)}, u32[]{:S(2)}) copy-start(f32[1536]{0:T(1024)} %get-tuple-element.52) | copy-start | bytes 18436
  2632.7 113.9 %copy-start.109 = (f32[64]{0:T(128)S(1)}, f32[64]{0:T(128)}, u32[]{:S(2)}) copy-start(f32[64]{0:T(128)} %get-tuple-element.46) | copy-start | bytes 772
  2632.7 113.9 %copy-start.112 = (f32[64]{0:T(128)S(1)}, f32[64]{0:T(128)}, u32[]{:S(2)}) copy-start(f32[64]{0:T(128)} %get-tuple-element.59) | copy-start | bytes 772
  2632.7 158.0 %copy-start.104 = (f32[196]{0:T(256)S(1)}, f32[196]{0:T(256)}, u32[]{:S(2)}) copy-start(f32[196]{0:T(256)} %param.17) | copy-start | bytes 2356
  2632.7 158.0 %copy-start.113 = (f32[196]{0:T(256)S(1)}, f32[196]{0:T(256)}, u32[]{:S(2)}) copy-start(f32[196]{0:T(256)} %param.19) | copy-start | bytes 2356
  2632.8 158.0 %copy-start.114 = (f32[196]{0:T(256)S(1)}, f32[196]{0:T(256)}, u32[]{:S(2)}) copy-start(f32[196]{0:T(256)} %param.18) | copy-start | bytes 2356
  2632.8 158.6 %copy-start.110 = (s32[6]{0:T(128)S(1)}, s32[6]{0:T(128)}, u32[]{:S(2)}) copy-start(s32[6]{0:T(128)} %constant.224) | copy-start | bytes 76
  2632.8 158.6 %copy-start.111 = (s32[6]{0:T(128)S(1)}, s32[6]{0:T(128)}, u32[]{:S(2)}) copy-start(s32[6]{0:T(128)} %constant.223) | copy-start | bytes 76
  2632.8 167.1 %copy-start.97 = (f32[160]{0:T(256)S(1)}, f32[160]{0:T(256)}, u32[]{:S(2)}) copy-start(f32[160]{0:T(256)} %copy-done.96) | copy-start | bytes 1924
  2632.8 167.1 %copy-start.31 = (f32[160,1536]{1,0:T(8,128)S(1)}, f32[160,1536]{1,0:T(8,128)}, u32[]{:S(2)}) copy-start(f32[160,1536]{1,0:T(8,128)} %get-tuple-element.85) | copy-start | bytes 2949124
  (103 other events, 914.5 us)
Sparse Core Ops, SparseCore 0:
  126.8 141.0 all-gather.32
  270.0 19.9 all-gather.16
  292.8 98.6 all-gather.36
  394.5 41.0 reduce-scatter.8
  437.6 605.7 all-gather.34
  1045.4 21.7 all-gather.18
  1127.4 42.9 reduce-scatter.10
  1172.9 21.8 all-gather.20
  1212.0 42.8 reduce-scatter.12
  1256.4 605.7 all-gather.38
  1864.3 21.7 all-gather.22
  1887.5 21.8 all-gather.24
  1969.7 42.9 reduce-scatter.16
  2018.5 21.8 all-gather.26
  2080.5 42.9 reduce-scatter.18
  2126.5 42.9 reduce-scatter.14
  2172.9 21.8 all-gather.28
  2222.1 42.8 reduce-scatter.20
  2394.2 22.1 all-gather.30
  2550.0 43.3 reduce-scatter.22
  2599.6 2313.7 all-reduce.20
where the time goes:
time: 5430 us; the launch traced here: 5390 us
  waiting for transfers between devices  3780 us (70%)
  local copies, waits for them, and re-layouts  747 us (14%)
  other arithmetic  485 us (9%)
  matrix products  234 us (4%)
  blocking collectives  130 us (2%)
    unnamed x22, waiting for transfers between devices  2110 us
    all_gather x4, waiting for transfers between devices, fetch_segment(): lax.all_gather(shard_part.astype(jnp.bfloat16).reshape(1, -1), 'dp', axis...  1370 us
    unnamed x287, local copies, waits for them, and re-layouts  318 us
    reduce_scatter x4, waiting for transfers between devices, sum_branch(): lax.psum_scatter(dot_rows(lhs_rows, rhs_matrix), 'tensor', scatter_dimens...  159 us
    concatenate x3, local copies, waits for them, and re-layouts, local(): grad_local = jnp.concatenate([grad_part for grad_part in reduced])  155 us
    mul x1, other arithmetic, adam_terms(): update = first_new / (jnp.sqrt(second_new) + ADAM_EPS) + DECAY * weight  116 us
    mul x1, other arithmetic, adam_terms(): BETA_SECOND * second_old + (1.0 - BETA_SECOND) * grad_vals * grad_vals  112 us
  transfers between devices with their start and end apart: 21, of which 14 were waited for; matrix products, arithmetic and copies ran while one was open for 14% of the time, Pallas kernels for 0%

commit v1 on v0

v1 whole, which is shorter than its diff:
```python
import math

import jax
import jax.numpy as jnp
import numpy as np
from jax import lax
from jax.experimental import pallas as pl
from jax.experimental.pallas import tpu as pltpu
from jax.sharding import PartitionSpec as P

MODEL_DIM = 1536
FEED_HIDDEN = 6912
QUERY_HEADS = 24
KEY_VALUE_HEADS = 8
HEAD_DIM = 64


NORM_EPS = 1e-05
ROPE_BASE = 1000000.0
BETA_FIRST = 0.9
BETA_SECOND = 0.99
ADAM_EPS = 1e-06
DECAY = 0.01
LEARN_RATE = 0.25
TRUST_EPS = 1e-06
MASK_FILL = -1e30


def weight_layout(model_width, conv_width, hidden_width, query_width, key_value_width):
    feed_shapes = [
        (model_width, hidden_width),
        (model_width, hidden_width),
        (hidden_width, model_width),
    ]
    return [
        [(model_width, 3, conv_width), (3, conv_width), (conv_width, model_width)],
        feed_shapes,
        [
            (model_width, query_width),
            (model_width, key_value_width),
            (model_width, key_value_width),
            (query_width, model_width),
        ],
        feed_shapes,
    ]


def rms_norm(values, gain_vec):
    return (
        values * lax.rsqrt(jnp.mean(values * values, axis=-1, keepdims=True) + NORM_EPS) * gain_vec
    )


def rotate(values, cosines, sines):
    half_dim = values.shape[-1] // 2
    first_half = values[..., :half_dim]
    second_half = values[..., half_dim:]
    return jnp.concatenate(
        [first_half * cosines - second_half * sines, second_half * cosines + first_half * sines],
        axis=-1,
    )


def head_prep(raw_rows, gain_vec, cosines, sines):
    sequence_length = raw_rows.shape[0]
    return rotate(
        rms_norm(raw_rows.reshape(sequence_length, -1, HEAD_DIM), gain_vec), cosines, sines
    )


def gated_unit(gate_vals, up_vals):
    return jax.nn.silu(gate_vals) * up_vals


def adam_terms(weight, grad_vals, first_old, second_old):
    first_new = BETA_FIRST * first_old + (1.0 - BETA_FIRST) * grad_vals
    second_new = BETA_SECOND * second_old + (1.0 - BETA_SECOND) * grad_vals * grad_vals
    update = first_new / (jnp.sqrt(second_new) + ADAM_EPS) + DECAY * weight
    return (first_new, second_new, update)


def dot_rows(lhs_rows, rhs_matrix):
    return jnp.dot(lhs_rows, rhs_matrix, preferred_element_type=jnp.float32)


def dot_first(lhs_rows, rhs_rows):
    return lax.dot_general(
        lhs_rows, rhs_rows, (((0,), (0,)), ((), ())), preferred_element_type=jnp.float32
    )


def dot_last(lhs_rows, rhs_matrix):
    return lax.dot_general(
        lhs_rows, rhs_matrix, (((1,), (1,)), ((), ())), preferred_element_type=jnp.float32
    )


def norm_back(values, gain_vec, grad_out):
    primal_out, pullback = jax.vjp(rms_norm, values, gain_vec)
    return pullback(grad_out)


TENSOR_ORDER = (0, 2, 1, 3)


def swap(values, axis_name, bit):
    count = lax.axis_size(axis_name)
    return lax.ppermute(values, axis_name, [(i, i ^ bit) for i in range(count)])


def gather_rows(values):
    if lax.axis_size("tensor") != 4:
        return lax.all_gather(values, "tensor", axis=0, tiled=True)
    far = swap(values, "tensor", 2)
    near = swap(values, "tensor", 1)
    return jnp.concatenate([values, far, near, swap(far, "tensor", 1)], axis=0)


def scatter_rows(partial):
    if lax.axis_size("tensor") != 4:
        return lax.psum_scatter(
            partial.astype(jnp.float32), "tensor", scatter_dimension=0, tiled=True
        )
    own, far, near, cross = jnp.split(partial, 4, axis=0)
    far_sum = far.astype(jnp.float32) + swap(cross, "tensor", 1).astype(jnp.float32)
    far_in = swap(far_sum.astype(partial.dtype), "tensor", 2)
    own_sum = own.astype(jnp.float32) + swap(near, "tensor", 1).astype(jnp.float32)
    return own_sum + far_in.astype(jnp.float32)


def block_owners():
    count = lax.axis_size("tensor")
    own = lax.axis_index("tensor")
    return jnp.stack([own ^ bit for bit in TENSOR_ORDER]) if count == 4 else jnp.arange(count)


def gather_sum(lhs_rows, rhs_matrix, send_type=jnp.float32):
    return scatter_rows(dot_rows(lhs_rows, rhs_matrix).astype(send_type))


def sum_input_grads(grad_pairs):
    running = None
    for grad_block, weight in grad_pairs:
        product_part = dot_last(grad_block, weight)
        running = product_part if running is None else running + product_part
    return scatter_rows(running.astype(jnp.bfloat16))


def flip_slots(slots, own):
    count = slots.shape[0]
    rest = slots.shape[1:]
    bit = 1
    while bit < count:
        view = slots.reshape((count // (2 * bit), 2, bit) + rest)
        slots = jnp.where((own & bit) != 0, view[:, ::-1], view).reshape((count,) + rest)
        bit *= 2
    return slots


def gather_small(values, axis_name):
    count = lax.axis_size(axis_name)
    slots = [values] + [swap(values, axis_name, bit) for bit in range(1, count)]
    return flip_slots(jnp.stack(slots), lax.axis_index(axis_name))


def scatter_small(values, axis_name):
    count = lax.axis_size(axis_name)
    slots = flip_slots(values, lax.axis_index(axis_name))
    total = slots[0]
    for bit in range(1, count):
        total = total + swap(slots[bit], axis_name, bit)
    return total


def sum_small(values):
    for axis_name in ("tensor", "dp"):
        values = jnp.sum(gather_small(values, axis_name), axis=0)
    return values


def shift_pairs(step):
    return [(z * 2 + y, (z + step) % 4 * 2 + y) for z in range(4) for y in range(2)]


def fetch_matrix(piece):
    if lax.axis_size("dp") != 8:
        whole = lax.all_gather(piece, "dp", axis=0, tiled=True)
        return whole, ()
    own = lax.axis_index("dp")
    z_own, y_own = own // 2, own % 2
    column = [piece] + [lax.ppermute(piece, "dp", shift_pairs(step)) for step in (1, 2, 3)]
    whole = jnp.zeros((8,) + piece.shape, piece.dtype)
    for step in range(4):
        slot = (z_own + 4 - step) % 4 * 2
        whole = lax.dynamic_update_index_in_dim(whole, column[step], slot + y_own, 0)
        other = swap(column[step], "dp", 1)
        whole = lax.dynamic_update_index_in_dim(whole, other, slot + 1 - y_own, 0)
    return whole.reshape((-1,) + piece.shape[1:]), tuple(column[1:])


def reduce_matrix(grad):
    dp_count = lax.axis_size("dp")
    if dp_count != 8:
        return lax.psum_scatter(grad.astype(jnp.float32), "dp", scatter_dimension=0, tiled=True)
    own = lax.axis_index("dp")
    z_own, y_own = own // 2, own % 2
    blocks = grad.astype(jnp.bfloat16).reshape((4, 2, grad.shape[0] // 8, grad.shape[1]))

    def block(slot, side):
        return lax.dynamic_slice(
            blocks, (slot, side, 0, 0), (1, 1) + blocks.shape[2:]
        ).reshape(blocks.shape[2:])

    total = None
    for step in (1, 2, 3, 0):
        slot = (z_own + step) % 4
        other = swap(block(slot, 1 - y_own), "dp", 1)
        pair = block(slot, y_own).astype(jnp.float32) + other.astype(jnp.float32)
        if step:
            pair = lax.ppermute(pair.astype(jnp.bfloat16), "dp", shift_pairs(step))
            pair = pair.astype(jnp.float32)
        total = pair if total is None else total + pair
    return total


def fetch_all(pieces):
    result = []
    landed = []
    for number, piece in enumerate(pieces):
        if number >= 2 and landed[number - 2]:
            piece, _ = lax.optimization_barrier((piece, landed[number - 2]))
        whole, hops = fetch_matrix(piece)
        landed.append(hops)
        result.append(whole)
    return result


class FlatPlan:
    def __init__(self, spans):
        self.total = sum(spans)
        self.gap = spans[1]
        self.gap_rows, self.gap_lanes = divmod(self.gap, 128)
        self.front = spans[0] // 128
        self.rows = self.front // 3
        self.rest = sum(spans[2:]) // 128
        self.front_blocks = 3
        self.blocks = 3 + -(-(self.rest + self.gap_rows + 1) // self.rows)
        sizes = [spans[0] // 128] + [span // 128 for span in spans[2:]]
        unit = math.gcd(*sizes)
        unit = math.gcd(unit, self.rows)
        while unit % 16 == 0 and unit > 128:
            unit //= 2
        self.unit = unit
        count = len(spans)
        per_block = self.rows // unit
        main = np.full(self.blocks * per_block, count, np.int32)
        edge = np.full(self.blocks * per_block, count, np.int32)
        front_units = self.front // unit
        main[:front_units] = 0
        at = front_units
        edge[at] = 1
        for number in range(2, count):
            units = spans[number] // 128 // unit
            main[at : at + units] = number
            edge[at + 1 : at + units + 1] = number
            at += units
        self.table = np.stack([main, edge])
        self.per_block = per_block
        self.count = count


def flat_spec(plan):
    return pl.BlockSpec((1, 1, plan.rows * 128), lambda i, *_: (0, 0, i))


def rows_spec(plan):
    return pl.BlockSpec((plan.rows, 128), lambda i, *_: (i, 0))


def lane_ids(rows):
    return lax.broadcasted_iota(jnp.int32, (rows, 128), 1)


def to_rows(plan, flat):
    rows, lanes, skip = plan.rows, plan.gap_lanes, plan.gap_rows
    last = -(-plan.total // 1024) - 1

    def body(cur_ref, next_ref, out_ref, work_ref):
        cur = cur_ref[0, 0].reshape(rows, 128)
        work_ref[0:rows, :] = cur
        work_ref[rows : rows + 8, :] = next_ref[0, 0].reshape(8, 128)
        low = pltpu.roll(work_ref[skip : skip + rows, :], 128 - lanes, 1)
        high = pltpu.roll(work_ref[skip + 1 : skip + 1 + rows, :], 128 - lanes, 1)
        moved = jnp.where(lane_ids(rows) < 128 - lanes, low, high)
        front = pl.program_id(0) < plan.front_blocks
        out_ref[...] = jnp.where(front, cur, moved).astype(jnp.bfloat16)

    return pl.pallas_call(
        body,
        name="to_rows",
        grid=(plan.blocks,),
        out_shape=jax.ShapeDtypeStruct((plan.blocks * rows, 128), jnp.bfloat16),
        in_specs=[
            flat_spec(plan),
            pl.BlockSpec(
                (1, 1, 1024), lambda i: (0, 0, jnp.minimum((i + 1) * (rows // 8), last))
            ),
        ],
        out_specs=rows_spec(plan),
        scratch_shapes=[pltpu.VMEM((rows + 8, 128), jnp.float32)],
        cost_estimate=pl.CostEstimate(
            flops=plan.total, bytes_accessed=6 * plan.total, transcendentals=0
        ),
    )(flat, flat)


def edge_mask(plan):
    place = lax.broadcasted_iota(jnp.int32, (8, 128), 0) * 128 + lane_ids(8)
    return (place < plan.gap) & (pl.program_id(0) >= plan.front_blocks)


def moments_pass(plan, weight, first_old, second_old, grad_rows, gap_rows):
    rows, lanes, skip, unit = plan.rows, plan.gap_lanes, plan.gap_rows, plan.unit

    def body(
        table, w_ref, m_ref, v_ref, g_ref, prev_ref, gap_ref,
        grad_ref, first_ref, second_ref, sums_ref, work_ref,
    ):
        step = pl.program_id(0)

        @pl.when(step == 0)
        def _():
            sums_ref[...] = jnp.zeros_like(sums_ref)

        cur = g_ref[...]
        prev = jnp.where(step == plan.front_blocks, gap_ref[...], prev_ref[...])
        work_ref[0:8, :] = pltpu.roll(prev, lanes, 1)
        work_ref[8 : 8 + rows, :] = pltpu.roll(cur, lanes, 1)
        low = work_ref[7 - skip : 7 - skip + rows, :]
        high = work_ref[8 - skip : 8 - skip + rows, :]
        moved = jnp.where(lane_ids(rows) < lanes, low, high)
        grad = jnp.where(step < plan.front_blocks, cur, moved)
        w = w_ref[0, 0].reshape(rows, 128)
        first_new, second_new, update = adam_terms(
            w, grad, m_ref[0, 0].reshape(rows, 128), v_ref[0, 0].reshape(rows, 128)
        )
        grad_ref[0, 0] = grad.reshape(rows * 128)
        first_ref[0, 0] = first_new.reshape(rows * 128)
        second_ref[0, 0] = second_new.reshape(rows * 128)
        mask = edge_mask(plan)
        for part in range(plan.per_block):
            main = table[0, step * plan.per_block + part]
            edge = table[1, step * plan.per_block + part]
            for base, values in ((0, w), (plan.count + 1, update)):
                square = values[part * unit : (part + 1) * unit]
                square = square * square
                inner = jnp.where(mask, 0.0, square[0:8])
                for at in range(8, unit, 8):
                    inner = inner + square[at : at + 8]
                sums_ref[base + main] += inner
                sums_ref[base + edge] += jnp.where(mask, square[0:8], 0.0)

    lin = flat_spec(plan)
    flat = jax.ShapeDtypeStruct((1, 1, plan.total), jnp.float32)
    sums = 2 * (plan.count + 1)
    return pl.pallas_call(
        body,
        name="moments_pass",
        grid_spec=pltpu.PrefetchScalarGridSpec(
            num_scalar_prefetch=1,
            grid=(plan.blocks,),
            in_specs=[
                lin, lin, lin, rows_spec(plan),
                pl.BlockSpec(
                    (8, 128), lambda i, *_: (jnp.maximum(i * (rows // 8) - 1, 0), 0)
                ),
                pl.BlockSpec((8, 128), lambda i, *_: (0, 0)),
            ],
            out_specs=[lin, lin, lin, pl.BlockSpec((sums, 8, 128), lambda i, *_: (0, 0, 0))],
            scratch_shapes=[pltpu.VMEM((rows + 8, 128), jnp.float32)],
        ),
        out_shape=[flat, flat, flat, jax.ShapeDtypeStruct((sums, 8, 128), jnp.float32)],
        cost_estimate=pl.CostEstimate(
            flops=20 * plan.total, bytes_accessed=28 * plan.total, transcendentals=plan.total
        ),
    )(jnp.asarray(plan.table), weight, first_old, second_old, grad_rows, grad_rows, gap_rows)


def weights_pass(plan, weight, first_new, second_new, ratios):
    rows, unit = plan.rows, plan.unit

    def body(table, w_ref, m_ref, v_ref, ratio_ref, new_ref, copy_ref):
        step = pl.program_id(0)
        mask = edge_mask(plan)
        pieces = []
        w = w_ref[0, 0].reshape(rows, 128)
        first, second = m_ref[0, 0].reshape(rows, 128), v_ref[0, 0].reshape(rows, 128)
        update = first / (jnp.sqrt(second) + ADAM_EPS) + DECAY * w
        for part in range(plan.per_block):
            main = ratio_ref[table[0, step * plan.per_block + part]]
            edge = ratio_ref[table[1, step * plan.per_block + part]]
            here = slice(part * unit, part * unit + 8)
            pieces.append(w[here] - LEARN_RATE * jnp.where(mask, edge, main) * update[here])
            here = slice(part * unit + 8, (part + 1) * unit)
            pieces.append(w[here] - LEARN_RATE * main * update[here])
        fresh = jnp.concatenate(pieces, axis=0)
        new_ref[0, 0] = fresh.reshape(rows * 128)
        copy_ref[0, 0] = fresh.reshape(rows * 128).astype(jnp.bfloat16)

    lin = flat_spec(plan)
    shape = (1, 1, plan.total)
    return pl.pallas_call(
        body,
        name="weights_pass",
        grid_spec=pltpu.PrefetchScalarGridSpec(
            num_scalar_prefetch=1,
            grid=(plan.blocks,),
            in_specs=[lin, lin, lin, pl.BlockSpec(memory_space=pltpu.SMEM)],
            out_specs=[lin, lin],
        ),
        out_shape=[
            jax.ShapeDtypeStruct(shape, jnp.float32),
            jax.ShapeDtypeStruct(shape, jnp.bfloat16),
        ],
        cost_estimate=pl.CostEstimate(
            flops=8 * plan.total, bytes_accessed=18 * plan.total, transcendentals=plan.total
        ),
    )(jnp.asarray(plan.table), weight, first_new, second_new, ratios)


def neighbour_rows(edge_rows, owners, offset):
    result = []
    for here in range(edge_rows.shape[0]):
        picked = jnp.zeros_like(edge_rows[0])
        for there in range(edge_rows.shape[0]):
            hit = owners[there] == owners[here] + offset
            picked = jnp.where(hit, edge_rows[there], picked)
        result.append(picked)
    return jnp.stack(result)


def mixer_forward(residual, gain_vec, weights, owners):
    w_in, kernel, w_out = weights
    conv_width = kernel.shape[1]
    normed_rows = gather_rows(rms_norm(residual, gain_vec).astype(jnp.bfloat16))
    projected = dot_rows(normed_rows, w_in).reshape(owners.shape[0], -1, 3 * conv_width)
    gate_b = projected[:, :, :conv_width]
    gate_c = projected[:, :, conv_width : 2 * conv_width]
    values = projected[:, :, 2 * conv_width :]
    product = gate_b * values
    padded = jnp.concatenate([neighbour_rows(product[:, -2:], owners, -1), product], axis=1)
    conv_mixed = (
        kernel[0] * padded[:, :-2] + kernel[1] * padded[:, 1:-1] + kernel[2] * padded[:, 2:]
    )
    conv_out = (gate_c * conv_mixed).astype(jnp.bfloat16).reshape(-1, conv_width)
    kept_vals = (normed_rows, gate_b, gate_c, values, padded, conv_mixed, conv_out)
    return (residual + gather_sum(conv_out, w_out), kept_vals)


def mixer_backward(grad_out, residual, gain_vec, weights, kept_vals, owners):
    w_in, kernel, w_out = weights
    normed_rows, gate_b, gate_c, values, padded, conv_mixed, conv_out = kept_vals
    grad_rows = gather_rows(grad_out.astype(jnp.bfloat16))
    d_conv = dot_last(grad_rows, w_out).reshape(conv_mixed.shape)
    d_gate_c = d_conv * conv_mixed
    d_mixed = d_conv * gate_c
    padded_grad = jnp.concatenate([d_mixed, neighbour_rows(d_mixed[:, :2], owners, 1)], axis=1)
    d_product = (
        kernel[0] * padded_grad[:, 2:]
        + kernel[1] * padded_grad[:, 1:-1]
        + kernel[2] * padded_grad[:, :-2]
    )
    d_kernel = jnp.stack(
        [
            jnp.sum(d_mixed * padded[:, :-2], axis=(0, 1)),
            jnp.sum(d_mixed * padded[:, 1:-1], axis=(0, 1)),
            jnp.sum(d_mixed * padded[:, 2:], axis=(0, 1)),
        ]
    )
    d_proj = jnp.concatenate(
        [
            (d_product * values).astype(jnp.bfloat16),
            d_gate_c.astype(jnp.bfloat16),
            (d_product * gate_b).astype(jnp.bfloat16),
        ],
        axis=-1,
    ).reshape(normed_rows.shape[0], -1)
    d_normed = sum_input_grads(((d_proj, w_in),))
    d_resid, d_gain = norm_back(residual, gain_vec, d_normed)
    grads = (grad_product(normed_rows, d_proj), grad_product(conv_out, grad_rows))
    return (grad_out + d_resid, d_gain, d_kernel, grads)


def grad_product(lhs_rows, rhs_rows):
    return reduce_matrix(dot_first(lhs_rows, rhs_rows).astype(jnp.bfloat16))


def ffn_forward(residual, gain_vec, weights, send_type=jnp.float32):
    w_gate, w_up, w_down = weights
    normed_rows = gather_rows(rms_norm(residual, gain_vec).astype(jnp.bfloat16))
    gate_vals = dot_rows(normed_rows, w_gate)
    up_vals = dot_rows(normed_rows, w_up)
    hidden = gated_unit(gate_vals, up_vals).astype(jnp.bfloat16)
    return (residual + gather_sum(hidden, w_down, send_type), (normed_rows, gate_vals, up_vals, hidden))


def ffn_backward(grad_out, residual, gain_vec, weights, kept_vals):
    w_gate, w_up, w_down = weights
    normed_rows, gate_vals, up_vals, hidden = kept_vals
    grad_rows = gather_rows(grad_out.astype(jnp.bfloat16))
    grad_down = grad_product(hidden, grad_rows)
    d_hidden = dot_last(grad_rows, w_down)
    primal_out, pullback = jax.vjp(gated_unit, gate_vals, up_vals)
    d_gate, d_up = pullback(d_hidden)
    d_gate = d_gate.astype(jnp.bfloat16)
    d_up = d_up.astype(jnp.bfloat16)
    d_normed = sum_input_grads(((d_gate, w_gate), (d_up, w_up)))
    d_resid, d_gain = norm_back(residual, gain_vec, d_normed)
    grads = (grad_product(normed_rows, d_gate), grad_product(normed_rows, d_up), grad_down)
    return (grad_out + d_resid, d_gain, grads)


def rope_tables_at(positions):
    inv_freq = ROPE_BASE ** (-jnp.arange(0, HEAD_DIM, 2, dtype=jnp.float32) / HEAD_DIM)
    angles = positions.astype(jnp.float32)[:, None] * inv_freq[None, :]
    return (jnp.cos(angles)[:, None, :], jnp.sin(angles)[:, None, :])


def score_block(query_b, key_b, causal):
    scores = jnp.einsum(
        "snge,tne->ngst", query_b, key_b, preferred_element_type=jnp.float32
    ) * HEAD_DIM ** (-0.5)
    return jnp.where(causal, scores, MASK_FILL)


def attention_forward(residual, gain_vec, gain_query, gain_key, weights, tables, causal):
    w_qkv, w_attn = weights
    cosines, sines = tables
    normed_rows = gather_rows(rms_norm(residual, gain_vec).astype(jnp.bfloat16))
    seq_len = normed_rows.shape[0]
    q_width = w_attn.shape[0]
    k_width = (w_qkv.shape[1] - q_width) // 2
    q_heads = q_width // HEAD_DIM
    kv_heads = k_width // HEAD_DIM
    projected = dot_rows(normed_rows, w_qkv)
    query_raw = projected[:, :q_width]
    key_raw = projected[:, q_width : q_width + k_width]
    value_b = (
        projected[:, q_width + k_width :]
        .astype(jnp.bfloat16)
        .reshape(seq_len, kv_heads, HEAD_DIM)
    )
    query_b = (
        head_prep(query_raw, gain_query, cosines, sines)
        .astype(jnp.bfloat16)
        .reshape(seq_len, kv_heads, q_heads // kv_heads, HEAD_DIM)
    )
    key_b = head_prep(key_raw, gain_key, cosines, sines).astype(jnp.bfloat16)
    scores = score_block(query_b, key_b, causal)
    top_score = jnp.max(scores, axis=-1, keepdims=True)
    exp_scores = jnp.exp(scores - top_score)
    exp_total = jnp.sum(exp_scores, axis=-1, keepdims=True)
    log_sum = top_score + jnp.log(exp_total)
    soft_probs = (exp_scores / exp_total).astype(jnp.bfloat16)
    attended = jnp.einsum("ngst,tne->snge", soft_probs, value_b, preferred_element_type=jnp.float32)
    attended = attended.reshape(seq_len, -1).astype(jnp.bfloat16)
    kept_vals = (normed_rows, query_raw, key_raw, query_b, key_b, value_b, log_sum, attended)
    return (residual + gather_sum(attended, w_attn), kept_vals)


def attention_backward(
    grad_out, residual, gain_vec, gain_query, gain_key, weights, tables, causal, kept_vals
):
    w_qkv, w_attn = weights
    cosines, sines = tables
    normed_rows, query_raw, key_raw, query_b, key_b, value_b, log_sum, attended = kept_vals
    seq_len = normed_rows.shape[0]
    grad_rows = gather_rows(grad_out.astype(jnp.bfloat16))
    grad_attn = grad_product(attended, grad_rows)
    d_attended = dot_last(grad_rows, w_attn).astype(jnp.bfloat16).reshape(query_b.shape)
    soft_probs = jnp.exp(score_block(query_b, key_b, causal) - log_sum)
    d_probs = jnp.einsum("snge,tne->ngst", d_attended, value_b, preferred_element_type=jnp.float32)
    d_value = jnp.einsum(
        "ngst,snge->tne",
        soft_probs.astype(jnp.bfloat16),
        d_attended,
        preferred_element_type=jnp.float32,
    )
    row_dot = jnp.sum(soft_probs * d_probs, axis=-1, keepdims=True)
    d_scores = (soft_probs * (d_probs - row_dot)).astype(jnp.bfloat16)
    score_scale = HEAD_DIM ** (-0.5)
    d_query = (
        jnp.einsum("ngst,tne->snge", d_scores, key_b, preferred_element_type=jnp.float32)
        * score_scale
    )
    d_key = (
        jnp.einsum("ngst,snge->tne", d_scores, query_b, preferred_element_type=jnp.float32)
        * score_scale
    )
    primal_query, pull_query = jax.vjp(
        lambda raw_rows, gain_vals: head_prep(raw_rows, gain_vals, cosines, sines),
        query_raw,
        gain_query,
    )
    d_query_raw, d_gain_query = pull_query(d_query.reshape(seq_len, -1, HEAD_DIM))
    primal_key, pull_key = jax.vjp(
        lambda raw_rows, gain_vals: head_prep(raw_rows, gain_vals, cosines, sines),
        key_raw,
        gain_key,
    )
    d_key_raw, d_gain_key = pull_key(d_key)
    d_qkv = jnp.concatenate(
        [
            d_query_raw.astype(jnp.bfloat16),
            d_key_raw.astype(jnp.bfloat16),
            d_value.reshape(seq_len, -1).astype(jnp.bfloat16),
        ],
        axis=1,
    )
    d_normed = sum_input_grads(((d_qkv, w_qkv),))
    d_resid, d_gain = norm_back(residual, gain_vec, d_normed)
    grads = (grad_product(normed_rows, d_qkv), grad_attn)
    return (grad_out + d_resid, d_gain, d_gain_query, d_gain_key, grads)


def local(
    tokens, cotangent, master, first_moment, second_moment, gain_master, gain_first, gain_second
):
    dp_count = lax.axis_size("dp")
    tensor_count = lax.axis_size("tensor")
    conv_width = MODEL_DIM // tensor_count
    hidden_width = FEED_HIDDEN // tensor_count
    q_width = QUERY_HEADS // tensor_count * HEAD_DIM
    k_width = KEY_VALUE_HEADS // tensor_count * HEAD_DIM
    mat_shapes = [
        mat_shape
        for segment in weight_layout(MODEL_DIM, conv_width, hidden_width, q_width, k_width)
        for mat_shape in segment
    ]
    spans = [math.prod(mat_shape) // dp_count for mat_shape in mat_shapes]
    plan = FlatPlan(spans)
    owners = block_owners()

    all_rows = to_rows(plan, master)
    pieces = []
    offset = 0
    for number, mat_shape in enumerate(mat_shapes):
        if number == 1:
            pieces.append(None)
            continue
        height = spans[number] // 128
        piece = all_rows[offset : offset + height]
        pieces.append(piece.reshape(mat_shape[0] // dp_count, -1))
        offset += height
    qkv_piece = jnp.concatenate(pieces[6:9], axis=1)

    gap_piece = master[0, 0, spans[0] : spans[0] + spans[1]]
    small = gather_small(jnp.concatenate([gap_piece, gain_master]), "dp")
    kernel = small[:, : spans[1]].reshape(mat_shapes[1])
    kernel = kernel.astype(jnp.bfloat16).astype(jnp.float32)
    gain_vector = gather_small(small[:, spans[1] :], "tensor").transpose(1, 0, 2).reshape(-1)

    gain_one = gain_vector[0:MODEL_DIM]
    gain_two = gain_vector[MODEL_DIM : 2 * MODEL_DIM]
    gain_three = gain_vector[2 * MODEL_DIM : 3 * MODEL_DIM]
    gain_four = gain_vector[3 * MODEL_DIM : 4 * MODEL_DIM]
    gain_query = gain_vector[4 * MODEL_DIM : 4 * MODEL_DIM + HEAD_DIM]
    gain_key = gain_vector[4 * MODEL_DIM + HEAD_DIM : 4 * MODEL_DIM + 2 * HEAD_DIM]

    w_in, w_out, gate_1, up_1, down_1, w_qkv, w_attn, gate_2, up_2, down_2 = fetch_all(
        [pieces[0], pieces[2], *pieces[3:6], qkv_piece, pieces[9], *pieces[10:13]]
    )

    rows_dev = tokens.shape[0]
    positions = (owners[:, None] * rows_dev + jnp.arange(rows_dev)[None, :]).reshape(-1)
    causal = positions[:, None] >= positions[None, :]
    tables = rope_tables_at(positions)

    resid_zero = tokens.astype(jnp.float32)
    mix_weights = (w_in, kernel, w_out)
    ffn_one = (gate_1, up_1, down_1)
    attn_weights = (w_qkv, w_attn)
    ffn_two = (gate_2, up_2, down_2)
    resid_one, kept_mix = mixer_forward(resid_zero, gain_one, mix_weights, owners)
    resid_two, kept_ffn_one = ffn_forward(resid_one, gain_two, ffn_one)
    resid_three, kept_attn = attention_forward(
        resid_two, gain_three, gain_query, gain_key, attn_weights, tables, causal
    )
    resid_four, kept_ffn_two = ffn_forward(
        resid_three, gain_four, ffn_two, jnp.bfloat16
    )

    grad_four = cotangent.astype(jnp.float32)
    grad_three, d_gain_four, grads_ffn_two = ffn_backward(
        grad_four, resid_three, gain_four, ffn_two, kept_ffn_two
    )
    grad_two, d_gain_three, d_gain_query, d_gain_key, grads_attn = attention_backward(
        grad_three,
        resid_two,
        gain_three,
        gain_query,
        gain_key,
        attn_weights,
        tables,
        causal,
        kept_attn,
    )
    grad_one, d_gain_two, grads_ffn_one = ffn_backward(
        grad_two, resid_one, gain_two, ffn_one, kept_ffn_one
    )
    grad_zero, d_gain_one, d_kernel, grads_mix = mixer_backward(
        grad_one, resid_zero, gain_one, mix_weights, kept_mix, owners
    )

    gain_partial = jnp.concatenate(
        [d_gain_one, d_gain_two, d_gain_three, d_gain_four, d_gain_query, d_gain_key]
    )
    gain_count = gain_master.shape[0]
    gain_partial = gain_partial.reshape(dp_count, tensor_count, gain_count).transpose(1, 0, 2)
    gain_column = scatter_small(gain_partial, "tensor")
    small_grad = scatter_small(
        jnp.concatenate([d_kernel.reshape(dp_count, -1), gain_column], axis=1), "dp"
    )
    gap_grad = small_grad[: spans[1]]
    gain_grad = small_grad[spans[1] :]

    grad_qkv, grad_attn = grads_attn
    grad_pieces = [
        grads_mix[0],
        grads_mix[1],
        *grads_ffn_one,
        grad_qkv[:, :q_width],
        grad_qkv[:, q_width : q_width + k_width],
        grad_qkv[:, q_width + k_width :],
        grad_attn,
        *grads_ffn_two,
    ]
    grad_rows = jnp.concatenate([piece.reshape(-1, 128) for piece in grad_pieces], axis=0)
    gap_rows = jnp.concatenate([jnp.zeros(1024 - spans[1], jnp.float32), gap_grad]).reshape(8, 128)
    grad_flat, first_new, second_new, squares = moments_pass(
        plan, master, first_moment, second_moment, grad_rows, gap_rows
    )
    square_sums = jnp.sum(squares, axis=(1, 2))
    mat_count = len(spans)
    weight_sq = square_sums[:mat_count]
    update_sq = square_sums[mat_count + 1 : 2 * mat_count + 1]

    gain_first_new, gain_second_new, gain_update = adam_terms(
        gain_master, gain_grad, gain_first, gain_second
    )
    positions = lax.axis_index(("dp", "tensor")) * gain_count + jnp.arange(
        gain_count, dtype=jnp.int32
    )
    gain_edges = jnp.asarray(
        np.cumsum([0, MODEL_DIM, MODEL_DIM, MODEL_DIM, MODEL_DIM, HEAD_DIM, HEAD_DIM]), jnp.int32
    )
    member = (
        (positions[:, None] >= gain_edges[None, :-1]) & (positions[:, None] < gain_edges[None, 1:])
    ).astype(jnp.float32)
    gain_wsq = jnp.sum((gain_master * gain_master)[:, None] * member, axis=0)
    gain_usq = jnp.sum((gain_update * gain_update)[:, None] * member, axis=0)
    totals = sum_small(jnp.concatenate([weight_sq, gain_wsq, update_sq, gain_usq]))
    norms = jnp.sqrt(totals.reshape(2, -1))
    trust_ratio = norms[0] / (norms[1] + TRUST_EPS)
    ratios = jnp.concatenate([trust_ratio[:mat_count], jnp.zeros(1, jnp.float32)])
    gain_ratio = jnp.sum(member * trust_ratio[None, mat_count:], axis=1)
    new_master, new_copy = weights_pass(plan, master, first_new, second_new, ratios)
    new_gain_master = gain_master - LEARN_RATE * gain_ratio * gain_update
    return (
        resid_four.astype(jnp.bfloat16),
        grad_zero,
        grad_flat,
        new_master,
        first_new,
        second_new,
        new_copy,
        gain_grad,
        new_gain_master,
        gain_first_new,
        gain_second_new,
        norms,
    )


def solution(mesh):
    in_specs = (
        P(("dp", "tensor"), None),
        P(("dp", "tensor"), None),
        P("tensor", "dp", None),
        P("tensor", "dp", None),
        P("tensor", "dp", None),
        P(("dp", "tensor")),
        P(("dp", "tensor")),
        P(("dp", "tensor")),
    )
    out_specs = (
        P(("dp", "tensor"), None),
        P(("dp", "tensor"), None),
        P("tensor", "dp", None),
        P("tensor", "dp", None),
        P("tensor", "dp", None),
        P("tensor", "dp", None),
        P("tensor", "dp", None),
        P(("dp", "tensor")),
        P(("dp", "tensor")),
        P(("dp", "tensor")),
        P(("dp", "tensor")),
        P(),
    )
    return jax.shard_map(local, mesh=mesh, in_specs=in_specs, out_specs=out_specs, check_vma=False)
```

time: 5430 us -> 1850 us (0.34)
  waiting for transfers between devices: 3780 us -> 789 us
  local copies, waits for them, and re-layouts: 747 us -> 188 us
  starting transfers between devices: 2.72 us -> 497 us
  other arithmetic: 485 us -> 83.7 us
  blocking collectives: 130 us -> 0 us
  Pallas kernels: 0 us -> 93.6 us
  matrix products: 234 us -> 179 us
    unnamed x22 -> x0, waiting for transfers between devices: 2110 us -> none
    all_gather x12 -> x0, waiting for transfers between devices: 1430 us -> none  [the longest x4 1370 us: fetch_segment(): lax.all_gather(shard_part.astype(jnp.bfloat16).reshape(1, -1), 'dp', axis...]
    ppermute x0 -> x218, waiting for transfers between devices: none -> 789 us  [the longest x158 480 us: swap(): return lax.ppermute(values, axis_name, [(i, i ^ bit) for i in range(count)])]
    ppermute x0 -> x218, starting transfers between devices: none -> 497 us  [the longest x30 232 us: reduce_matrix(): pair = lax.ppermute(pair.astype(jnp.bfloat16), 'dp', shift_pairs(step))]
    unnamed x287 -> x415, local copies, waits for them, and re-layouts: 318 us -> 28.2 us
    mul x3 -> x1, other arithmetic: 254 us -> 0.08 us  [local(): owners[:, None] * rows_dev + jnp.arange(rows_dev)[None, :]]
    reduce_scatter x8 -> x0, waiting for transfers between devices: 236 us -> none  [the longest x4 159 us: sum_branch(): lax.psum_scatter(dot_rows(lhs_rows, rhs_matrix), 'tensor', scatter_dimens...]
    concatenate x6 -> x4, local copies, waits for them, and re-layouts: 178 us -> 1.28 us  [the longest x1 1.15 us: local(): jnp.concatenate([piece.reshape(-1, 128) for piece in grad_pieces], axis=0)]
  transfers between devices with their start and end apart: 21 -> 218, of which waited for: 14 -> 86; matrix products, arithmetic and copies ran while one was open for 14% -> 19% of each run, Pallas kernels for 0% -> 1%
where the time goes in v1:
time: 1850 us; the launch traced here: 1830 us
  waiting for transfers between devices  789 us (43%)
  starting transfers between devices  497 us (27%)
  local copies, waits for them, and re-layouts  188 us (10%)
  matrix products  179 us (10%)
  Pallas kernels  93.6 us (5%)
  other arithmetic  83.7 us (5%)
    ppermute x158, waiting for transfers between devices, swap(): return lax.ppermute(values, axis_name, [(i, i ^ bit) for i in range(count)])  480 us
    ppermute x30, starting transfers between devices, reduce_matrix(): pair = lax.ppermute(pair.astype(jnp.bfloat16), 'dp', shift_pairs(step))  232 us
    ppermute x30, waiting for transfers between devices, fetch_matrix(): lax.ppermute(piece, 'dp', shift_pairs(step))  172 us
    ppermute x158, starting transfers between devices, swap(): return lax.ppermute(values, axis_name, [(i, i ^ bit) for i in range(count)])  144 us
    ppermute x30, waiting for transfers between devices, reduce_matrix(): pair = lax.ppermute(pair.astype(jnp.bfloat16), 'dp', shift_pairs(step))  137 us
    ppermute x30, starting transfers between devices, fetch_matrix(): lax.ppermute(piece, 'dp', shift_pairs(step))  121 us
    dot_general x10, matrix products, dot_rows(): return jnp.dot(lhs_rows, rhs_matrix, preferred_element_type=jnp.float32)  60.4 us
    dot_general x10, matrix products, dot_last(): lax.dot_general(lhs_rows, rhs_matrix, (((1,), (1,)), ((), ())), preferred...  50.5 us
  transfers between devices with their start and end apart: 218, of which 86 were waited for; matrix products, arithmetic and copies ran while one was open for 19% of the time, Pallas kernels for 1%

profile of v1, /device:TPU:0, one launch (start us, length us, event | category | flops | bytes accessed | tf_op | source)
XLA Modules:
  0.0 1834.0 jit_solution(1475525595935848375)
XLA Ops:
  11.5 21.8 %to_rows.1 = bf16[19584,128]{1,0:T(8,128)(2,1)} custom-call(f32[1,1,2482320]{2,1,0:T(1,128)} %w_ref.3, f32[1,1,2482320]{2,1,0:T(1,128)} %w_ref.3), custom_call_target="tpu_custom_call" | custom-call | flops 2482320 | bytes 14893920 | tf_op jit(solution)/shard_map/to_rows/pallas_call | solution.py:298
  86.1 13.3 collective-permute-done.21
  99.4 13.1 collective-permute-done.23
  171.3 29.2 %collective-permute-done.43 = bf16[192,1728]{1,0:T(8,128)(2,1)S(1)} collective-permute-done((bf16[192,1728]{1,0:T(8,128)(2,1)S(1)}, bf16[192,1728]{1,0:T(8,128)(2,1)S(1)}, u32[]{:S(2)}, u32[]{:S(2)}) %collective-permute-start.43) | collective-permute-done | bytes 663584 | tf_op jit(solution)/shard_map/ppermute | solution.py:191
  200.5 11.5 collective-permute-start.34
  214.4 10.8 collective-permute-done.15
  261.6 14.1 collective-permute-start.36
  275.7 20.9 %collective-permute-start.38 = (bf16[192,1728]{1,0:T(8,128)(2,1)S(1)}, bf16[192,1728]{1,0:T(8,128)(2,1)S(1)}, u32[]{:S(2)}, u32[]{:S(2)}) collective-permute-start(bf16[192,1728]{1,0:T(8,128)(2,1)S(1)} %reshape.762), channel_id=1, source_target_pairs={{0,24},{4,28},{8,0},{12,4},{16,8},{20,12},{24,16},{28,20},{1,25},{... | collective-permute-start | bytes 1990664 | tf_op jit(solution)/shard_map/ppermute | solution.py:191
  317.8 47.4 %collective-permute-done.62 = bf16[192,640]{1,0:T(8,128)(2,1)S(1)} collective-permute-done((bf16[192,640]{1,0:T(8,128)(2,1)S(1)}, bf16[192,640]{1,0:T(8,128)(2,1)S(1)}, u32[]{:S(2)}, u32[]{:S(2)}) %collective-permute-start.62) | collective-permute-done | bytes 245792 | tf_op jit(solution)/shard_map/ppermute | solution.py:108
  388.2 14.8 collective-permute-done.81
  404.7 33.4 %collective-permute-done.83 = bf16[192,1728]{1,0:T(8,128)(2,1)S(1)} collective-permute-done((bf16[192,1728]{1,0:T(8,128)(2,1)S(1)}, bf16[192,1728]{1,0:T(8,128)(2,1)S(1)}, u32[]{:S(2)}, u32[]{:S(2)}) %collective-permute-start.83) | collective-permute-done | bytes 663584 | tf_op jit(solution)/shard_map/ppermute | solution.py:191
  438.0 17.9 collective-permute-start.52
  458.2 16.0 collective-permute-done.50
  510.9 27.5 %collective-permute-done.69 = bf16[48,1536]{1,0:T(8,128)(2,1)S(1)} collective-permute-done((bf16[48,1536]{1,0:T(8,128)(2,1)S(1)}, bf16[48,1536]{1,0:T(8,128)(2,1)S(1)}, u32[]{:S(2)}, u32[]{:S(2)}) %collective-permute-start.69) | collective-permute-done | bytes 147488 | tf_op jit(solution)/shard_map/ppermute | solution.py:108
  553.1 12.0 collective-permute-done.84
  570.0 13.1 collective-permute-done.49
  605.5 15.2 collective-permute-done.53
  653.7 14.5 collective-permute-done.88
  674.7 12.8 collective-permute-done.99
  690.7 14.5 collective-permute-done.98
  741.6 14.8 collective-permute-done.76
  777.7 14.6 fusion.11
  867.3 13.9 collective-permute-done.184
  884.6 11.4 collective-permute-done.186
  896.0 14.7 collective-permute-done.188
  912.0 13.5 collective-permute-done.177
  926.2 14.0 collective-permute-done.179
  940.8 14.2 collective-permute-done.181
  955.0 14.6 collective-permute-start.192
  988.3 25.5 %collective-permute-start.187 = (bf16[192,1728]{1,0:T(8,128)(2,1)S(1)}, bf16[192,1728]{1,0:T(8,128)(2,1)S(1)}, u32[]{:S(2)}, u32[]{:S(2)}) collective-permute-start(bf16[192,1728]{1,0:T(8,128)(2,1)S(1)} %get-tuple-element.97), channel_id=1, source_target_pairs={{0,16},{4,20},{8,24},{12,28},{16,0},{20,4},{24,8},{28,12},{1,17},{... | collective-permute-start | bytes 1990664 | tf_op jit(solution)/shard_map/ppermute | solution.py:220
  1016.8 35.8 %collective-permute-start.189 = (bf16[192,1728]{1,0:T(8,128)(2,1)S(1)}, bf16[192,1728]{1,0:T(8,128)(2,1)S(1)}, u32[]{:S(2)}, u32[]{:S(2)}) collective-permute-start(bf16[192,1728]{1,0:T(8,128)(2,1)S(1)} %get-tuple-element.96), channel_id=1, source_target_pairs={{0,24},{4,28},{8,0},{12,4},{16,8},{20,12},{24,16},{28,20},{1,25},{... | collective-permute-start | bytes 1990664 | tf_op jit(solution)/shard_map/ppermute | solution.py:220
  1059.5 12.8 collective-permute-start.178
  1072.2 30.3 %collective-permute-done.187 = bf16[192,1728]{1,0:T(8,128)(2,1)S(1)} collective-permute-done((bf16[192,1728]{1,0:T(8,128)(2,1)S(1)}, bf16[192,1728]{1,0:T(8,128)(2,1)S(1)}, u32[]{:S(2)}, u32[]{:S(2)}) %collective-permute-start.187) | collective-permute-done | bytes 663584 | tf_op jit(solution)/shard_map/ppermute | solution.py:220
  1227.7 11.2 fusion.14
  1313.8 13.3 collective-permute-done.153
  1341.3 14.2 collective-permute-done.160
  1358.6 11.7 collective-permute-done.142
  1371.7 13.3 collective-permute-done.144
  1386.4 13.4 collective-permute-done.146
  1437.5 14.1 collective-permute-done.159
  1453.1 42.3 %collective-permute-start.143 = (bf16[192,1728]{1,0:T(8,128)(2,1)}, bf16[192,1728]{1,0:T(8,128)(2,1)}, u32[]{:S(2)}, u32[]{:S(2)}) collective-permute-start(bf16[192,1728]{1,0:T(8,128)(2,1)} %get-tuple-element.116), channel_id=1, source_target_pairs={{0,8},{4,12},{8,16},{12,20},{16,24},{20,28},{24,0},{28,4},{1,9},{5... | collective-permute-start | bytes 1990664 | tf_op jit(solution)/shard_map/ppermute | solution.py:220
  1495.4 14.3 collective-permute-start.145
  1509.6 27.8 %collective-permute-done.152 = bf16[192,1728]{1,0:T(8,128)(2,1)S(1)} collective-permute-done((bf16[192,1728]{1,0:T(8,128)(2,1)S(1)}, bf16[192,1728]{1,0:T(8,128)(2,1)S(1)}, u32[]{:S(2)}, u32[]{:S(2)}) %collective-permute-start.152) | collective-permute-done | bytes 663584 | tf_op jit(solution)/shard_map/ppermute | solution.py:220
  1553.0 14.1 collective-permute-done.145
  1609.2 12.2 collective-permute-start.136
  1674.8 15.8 collective-permute-done.131
  1737.7 39.7 %moments_pass.1 = (f32[1,1,2482320]{2,1,0:T(1,128)}, f32[1,1,2482320]{2,1,0:T(1,128)}, f32[1,1,2482320]{2,1,0:T(1,128)}, f32[28,8,128]{2,1,0:T(8,128)}) custom-call(s32[2,204]{1,0:T(2,128)} %constant.555.clone.table, f32[1,1,2482320]{2,1,0:T(1,128)} %w_ref.3, f32[1,1,2482320]{2,1,0:T(1,128)} %m_ref.1, f32[1,1,2482320]{2,1,0:T(1,128)} %v_ref.1, ...), custom_call_target="tpu_custom_call" | custom-call | flops 49646400 | bytes 69504960 | tf_op jit(solution)/shard_map/moments_pass/pallas_call | solution.py:366
  1801.7 32.1 %weights_pass.1 = (f32[1,1,2482320]{2,1,0:T(1,128)}, bf16[1,1,2482320]{2,1,0:T(2,128)(2,1)}) custom-call(s32[2,204]{1,0:T(2,128)} %constant.555.clone.table, f32[1,1,2482320]{2,1,0:T(1,128)} %w_ref.3, f32[1,1,2482320]{2,1,0:T(1,128)} %get-tuple-element.18.m_ref, f32[1,1,2482320]{2,1,0:T(1,128)} %get-tuple-element.19.v_ref, f32[14]{0:T(128)} %pad_maximum_fusion.28.ratio_ref), custom_call_target="tpu_custom_call" | custom-call | flops 19858560 | bytes 44681760 | tf_op jit(solution)/shard_map/weights_pass/pallas_call | solution.py:412
  (1167 shorter events, 936.1 us)
Async XLA Ops:
  2.7 61.5 %collective-permute-start = (f32[340]{0:T(512)}, f32[340]{0:T(512)}, u32[]{:S(2)}, u32[]{:S(2)}) collective-permute-start(f32[340]{0:T(512)} %pad_maximum_fusion.25), channel_id=1, source_target_pairs={{0,4},{4,0},{8,12},{12,8},{16,20},{20,16},{24,28},{28,24},{1,5},{5... | collective-permute-start | bytes 4088 | tf_op jit(solution)/shard_map/ppermute | solution.py:108
  5.7 62.1 %collective-permute-start.1 = (f32[340]{0:T(512)}, f32[340]{0:T(512)}, u32[]{:S(2)}, u32[]{:S(2)}) collective-permute-start(f32[340]{0:T(512)} %pad_maximum_fusion.25), channel_id=1, source_target_pairs={{0,8},{4,12},{8,0},{12,4},{16,24},{20,28},{24,16},{28,20},{1,9},{5... | collective-permute-start | bytes 4088 | tf_op jit(solution)/shard_map/ppermute | solution.py:108
  7.2 64.4 %collective-permute-start.2 = (f32[340]{0:T(512)}, f32[340]{0:T(512)}, u32[]{:S(2)}, u32[]{:S(2)}) collective-permute-start(f32[340]{0:T(512)} %pad_maximum_fusion.25), channel_id=1, source_target_pairs={{0,12},{4,8},{8,4},{12,0},{16,28},{20,24},{24,20},{28,16},{1,13},{... | collective-permute-start | bytes 4088 | tf_op jit(solution)/shard_map/ppermute | solution.py:108
  7.2 65.1 %collective-permute-start.3 = (f32[340]{0:T(512)}, f32[340]{0:T(512)}, u32[]{:S(2)}, u32[]{:S(2)}) collective-permute-start(f32[340]{0:T(512)} %pad_maximum_fusion.25), channel_id=1, source_target_pairs={{0,16},{4,20},{8,24},{12,28},{16,0},{20,4},{24,8},{28,12},{1,17},{... | collective-permute-start | bytes 4088 | tf_op jit(solution)/shard_map/ppermute | solution.py:108
  10.2 67.1 %collective-permute-start.4 = (f32[340]{0:T(512)}, f32[340]{0:T(512)}, u32[]{:S(2)}, u32[]{:S(2)}) collective-permute-start(f32[340]{0:T(512)} %pad_maximum_fusion.25), channel_id=1, source_target_pairs={{0,20},{4,16},{8,28},{12,24},{16,4},{20,0},{24,12},{28,8},{1,21},{... | collective-permute-start | bytes 4088 | tf_op jit(solution)/shard_map/ppermute | solution.py:108
  71.6 71.6 %collective-permute-start.14 = (bf16[192,1152]{1,0:T(8,128)(2,1)}, bf16[192,1152]{1,0:T(8,128)(2,1)}, u32[]{:S(2)}, u32[]{:S(2)}) collective-permute-start(bf16[192,1152]{1,0:T(8,128)(2,1)} %reshape.757), channel_id=1, source_target_pairs={{0,8},{4,12},{8,16},{12,20},{16,24},{20,28},{24,0},{28,4},{1,9},{5... | collective-permute-start | bytes 1327112 | tf_op jit(solution)/shard_map/ppermute | solution.py:191
  72.3 71.0 %collective-permute-start.16 = (bf16[192,1152]{1,0:T(8,128)(2,1)}, bf16[192,1152]{1,0:T(8,128)(2,1)}, u32[]{:S(2)}, u32[]{:S(2)}) collective-permute-start(bf16[192,1152]{1,0:T(8,128)(2,1)} %reshape.757), channel_id=1, source_target_pairs={{0,16},{4,20},{8,24},{12,28},{16,0},{20,4},{24,8},{28,12},{1,17},{... | collective-permute-start | bytes 1327112 | tf_op jit(solution)/shard_map/ppermute | solution.py:191
  155.9 56.1 %collective-permute-start.45 = (bf16[192,1728]{1,0:T(8,128)(2,1)S(1)}, bf16[192,1728]{1,0:T(8,128)(2,1)S(1)}, u32[]{:S(2)}, u32[]{:S(2)}) collective-permute-start(bf16[192,1728]{1,0:T(8,128)(2,1)S(1)} %copy-done.44), channel_id=1, source_target_pairs={{0,24},{4,28},{8,0},{12,4},{16,8},{20,12},{24,16},{28,20},{1,25},{... | collective-permute-start | bytes 1990664 | tf_op jit(solution)/shard_map/ppermute | solution.py:191
  160.2 69.2 %collective-permute-start.10 = (bf16[160,1536]{1,0:T(8,128)(2,1)S(1)}, bf16[160,1536]{1,0:T(8,128)(2,1)S(1)}, u32[]{:S(2)}, u32[]{:S(2)}) collective-permute-start(bf16[160,1536]{1,0:T(8,128)(2,1)S(1)} %fusion.52), channel_id=1, source_target_pairs={{0,2},{1,3},{2,0},{3,1},{4,6},{5,7},{6,4},{7,5},{8,10},{9,11},{10,... | collective-permute-start | bytes 1474568 | tf_op jit(solution)/shard_map/ppermute | solution.py:108
  171.3 78.2 %collective-permute-start.11 = (bf16[160,1536]{1,0:T(8,128)(2,1)S(1)}, bf16[160,1536]{1,0:T(8,128)(2,1)S(1)}, u32[]{:S(2)}, u32[]{:S(2)}) collective-permute-start(bf16[160,1536]{1,0:T(8,128)(2,1)S(1)} %fusion.52), channel_id=1, source_target_pairs={{0,1},{1,0},{2,3},{3,2},{4,5},{5,4},{6,7},{7,6},{8,9},{9,8},{10,11... | collective-permute-start | bytes 1474568 | tf_op jit(solution)/shard_map/ppermute | solution.py:108
  200.5 98.7 %collective-permute-start.34 = (bf16[192,1728]{1,0:T(8,128)(2,1)S(1)}, bf16[192,1728]{1,0:T(8,128)(2,1)}, u32[]{:S(2)}, u32[]{:S(2)}) collective-permute-start(bf16[192,1728]{1,0:T(8,128)(2,1)S(1)} %reshape.762), channel_id=1, source_target_pairs={{0,8},{4,12},{8,16},{12,20},{16,24},{20,28},{24,0},{28,4},{1,9},{5... | collective-permute-start | bytes 1990664 | tf_op jit(solution)/shard_map/ppermute | solution.py:191
  297.1 85.5 %collective-permute-start.42 = (bf16[192,1728]{1,0:T(8,128)(2,1)S(1)}, bf16[192,1728]{1,0:T(8,128)(2,1)S(1)}, u32[]{:S(2)}, u32[]{:S(2)}) collective-permute-start(bf16[192,1728]{1,0:T(8,128)(2,1)S(1)} %collective-permute-done.41), channel_id=1, source_target_pairs={{0,4},{4,0},{8,12},{12,8},{16,20},{20,16},{24,28},{28,24},{1,5},{5... | collective-permute-start | bytes 1990664 | tf_op jit(solution)/shard_map/ppermute | solution.py:108
  299.2 83.6 %collective-permute-start.44 = (bf16[192,1728]{1,0:T(8,128)(2,1)S(1)}, bf16[192,1728]{1,0:T(8,128)(2,1)S(1)}, u32[]{:S(2)}, u32[]{:S(2)}) collective-permute-start(bf16[192,1728]{1,0:T(8,128)(2,1)S(1)} %collective-permute-done.43), channel_id=1, source_target_pairs={{0,4},{4,0},{8,12},{12,8},{16,20},{20,16},{24,28},{28,24},{1,5},{5... | collective-permute-start | bytes 1990664 | tf_op jit(solution)/shard_map/ppermute | solution.py:108
  299.8 87.1 %collective-permute-start.46 = (bf16[192,1728]{1,0:T(8,128)(2,1)S(1)}, bf16[192,1728]{1,0:T(8,128)(2,1)S(1)}, u32[]{:S(2)}, u32[]{:S(2)}) collective-permute-start(bf16[192,1728]{1,0:T(8,128)(2,1)S(1)} %collective-permute-done.45), channel_id=1, source_target_pairs={{0,4},{4,0},{8,12},{12,8},{16,20},{20,16},{24,28},{28,24},{1,5},{5... | collective-permute-start | bytes 1990664 | tf_op jit(solution)/shard_map/ppermute | solution.py:108
  305.9 81.6 %collective-permute-start.80 = (bf16[192,1728]{1,0:T(8,128)(2,1)S(1)}, bf16[192,1728]{1,0:T(8,128)(2,1)S(1)}, u32[]{:S(2)}, u32[]{:S(2)}) collective-permute-start(bf16[192,1728]{1,0:T(8,128)(2,1)S(1)} %reshape.775), channel_id=1, source_target_pairs={{0,4},{4,0},{8,12},{12,8},{16,20},{20,16},{24,28},{28,24},{1,5},{5... | collective-permute-start | bytes 1990664 | tf_op jit(solution)/shard_map/ppermute | solution.py:108
  386.8 87.9 %collective-permute-start.47 = (bf16[216,1536]{1,0:T(8,128)(2,1)S(1)}, bf16[216,1536]{1,0:T(8,128)(2,1)}, u32[]{:S(2)}, u32[]{:S(2)}) collective-permute-start(bf16[216,1536]{1,0:T(8,128)(2,1)S(1)} %copy-done.45), channel_id=1, source_target_pairs={{0,4},{4,0},{8,12},{12,8},{16,20},{20,16},{24,28},{28,24},{1,5},{5... | collective-permute-start | bytes 1990664 | tf_op jit(solution)/shard_map/ppermute | solution.py:108
  387.5 70.6 %collective-permute-start.48 = (bf16[216,1536]{1,0:T(8,128)(2,1)S(1)}, bf16[216,1536]{1,0:T(8,128)(2,1)}, u32[]{:S(2)}, u32[]{:S(2)}) collective-permute-start(bf16[216,1536]{1,0:T(8,128)(2,1)S(1)} %copy-done.45), channel_id=1, source_target_pairs={{0,8},{4,12},{8,16},{12,20},{16,24},{20,28},{24,0},{28,4},{1,9},{5... | collective-permute-start | bytes 1990664 | tf_op jit(solution)/shard_map/ppermute | solution.py:191
  474.2 121.5 %collective-permute-start.27 = (f32[160,1536]{1,0:T(8,128)S(1)}, f32[160,1536]{1,0:T(8,128)S(1)}, u32[]{:S(2)}, u32[]{:S(2)}) collective-permute-start(f32[160,1536]{1,0:T(8,128)S(1)} %get-tuple-element.152), channel_id=1, source_target_pairs={{0,1},{1,0},{2,3},{3,2},{4,5},{5,4},{6,7},{7,6},{8,9},{9,8},{10,11... | collective-permute-start | bytes 2949128 | tf_op jit(solution)/shard_map/ppermute | solution.py:108
  504.0 62.5 %collective-permute-start.94 = (bf16[216,1536]{1,0:T(8,128)(2,1)}, bf16[216,1536]{1,0:T(8,128)(2,1)}, u32[]{:S(2)}, u32[]{:S(2)}) collective-permute-start(bf16[216,1536]{1,0:T(8,128)(2,1)} %reshape.779), channel_id=1, source_target_pairs={{0,4},{4,0},{8,12},{12,8},{16,20},{20,16},{24,28},{28,24},{1,5},{5... | collective-permute-start | bytes 1990664 | tf_op jit(solution)/shard_map/ppermute | solution.py:108
  504.6 144.0 %collective-permute-start.95 = (bf16[216,1536]{1,0:T(8,128)(2,1)}, bf16[216,1536]{1,0:T(8,128)(2,1)}, u32[]{:S(2)}, u32[]{:S(2)}) collective-permute-start(bf16[216,1536]{1,0:T(8,128)(2,1)} %reshape.779), channel_id=1, source_target_pairs={{0,8},{4,12},{8,16},{12,20},{16,24},{20,28},{24,0},{28,4},{1,9},{5... | collective-permute-start | bytes 1990664 | tf_op jit(solution)/shard_map/ppermute | solution.py:191
  549.6 120.9 %collective-permute-start.97 = (bf16[216,1536]{1,0:T(8,128)(2,1)}, bf16[216,1536]{1,0:T(8,128)(2,1)S(1)}, u32[]{:S(2)}, u32[]{:S(2)}) collective-permute-start(bf16[216,1536]{1,0:T(8,128)(2,1)} %reshape.779), channel_id=1, source_target_pairs={{0,16},{4,20},{8,24},{12,28},{16,0},{20,4},{24,8},{28,12},{1,17},{... | collective-permute-start | bytes 1990664 | tf_op jit(solution)/shard_map/ppermute | solution.py:191
  594.4 56.1 %collective-permute-start.86 = (bf16[192,1728]{1,0:T(8,128)(2,1)}, bf16[192,1728]{1,0:T(8,128)(2,1)S(1)}, u32[]{:S(2)}, u32[]{:S(2)}) collective-permute-start(bf16[192,1728]{1,0:T(8,128)(2,1)} %collective-permute-done.85), channel_id=1, source_target_pairs={{0,4},{4,0},{8,12},{12,8},{16,20},{20,16},{24,28},{28,24},{1,5},{5... | collective-permute-start | bytes 1990664 | tf_op jit(solution)/shard_map/ppermute | solution.py:108
  864.3 61.2 %collective-permute-start.177 = (bf16[192,1728]{1,0:T(8,128)(2,1)S(1)}, bf16[192,1728]{1,0:T(8,128)(2,1)S(1)}, u32[]{:S(2)}, u32[]{:S(2)}) collective-permute-start(bf16[192,1728]{1,0:T(8,128)(2,1)S(1)} %get-tuple-element.105), channel_id=1, source_target_pairs={{0,4},{4,0},{8,12},{12,8},{16,20},{20,16},{24,28},{28,24},{1,5},{5... | collective-permute-start | bytes 1990664 | tf_op jit(solution)/shard_map/ppermute | solution.py:108
  866.6 73.6 %collective-permute-start.179 = (bf16[192,1728]{1,0:T(8,128)(2,1)S(1)}, bf16[192,1728]{1,0:T(8,128)(2,1)S(1)}, u32[]{:S(2)}, u32[]{:S(2)}) collective-permute-start(bf16[192,1728]{1,0:T(8,128)(2,1)S(1)} %get-tuple-element.108), channel_id=1, source_target_pairs={{0,4},{4,0},{8,12},{12,8},{16,20},{20,16},{24,28},{28,24},{1,5},{5... | collective-permute-start | bytes 1990664 | tf_op jit(solution)/shard_map/ppermute | solution.py:108
  881.3 73.7 %collective-permute-start.181 = (bf16[192,1728]{1,0:T(8,128)(2,1)S(1)}, bf16[192,1728]{1,0:T(8,128)(2,1)S(1)}, u32[]{:S(2)}, u32[]{:S(2)}) collective-permute-start(bf16[192,1728]{1,0:T(8,128)(2,1)S(1)} %get-tuple-element.107), channel_id=1, source_target_pairs={{0,4},{4,0},{8,12},{12,8},{16,20},{20,16},{24,28},{28,24},{1,5},{5... | collective-permute-start | bytes 1990664 | tf_op jit(solution)/shard_map/ppermute | solution.py:108
  910.8 58.9 %collective-permute-start.109 = (bf16[160,1536]{1,0:T(8,128)(2,1)S(1)}, bf16[160,1536]{1,0:T(8,128)(2,1)S(1)}, u32[]{:S(2)}, u32[]{:S(2)}) collective-permute-start(bf16[160,1536]{1,0:T(8,128)(2,1)S(1)} %add_convert_fusion.5), channel_id=1, source_target_pairs={{0,2},{1,3},{2,0},{3,1},{4,6},{5,7},{6,4},{7,5},{8,10},{9,11},{10,... | collective-permute-start | bytes 1474568 | tf_op jit(solution)/shard_map/ppermute | solution.py:108
  911.9 63.8 %collective-permute-start.101 = (bf16[160,1536]{1,0:T(8,128)(2,1)S(1)}, bf16[160,1536]{1,0:T(8,128)(2,1)S(1)}, u32[]{:S(2)}, u32[]{:S(2)}) collective-permute-start(bf16[160,1536]{1,0:T(8,128)(2,1)S(1)} %copy-done.100), channel_id=1, source_target_pairs={{0,1},{1,0},{2,3},{3,2},{4,5},{5,4},{6,7},{7,6},{8,9},{9,8},{10,11... | collective-permute-start | bytes 1474568 | tf_op jit(solution)/shard_map/ppermute | solution.py:108
  975.7 83.2 %collective-permute-start.190 = (bf16[192,1728]{1,0:T(8,128)(2,1)S(1)}, bf16[192,1728]{1,0:T(8,128)(2,1)S(1)}, u32[]{:S(2)}, u32[]{:S(2)}) collective-permute-start(bf16[192,1728]{1,0:T(8,128)(2,1)S(1)} %get-tuple-element.99), channel_id=1, source_target_pairs={{0,4},{4,0},{8,12},{12,8},{16,20},{20,16},{24,28},{28,24},{1,5},{5... | collective-permute-start | bytes 1990664 | tf_op jit(solution)/shard_map/ppermute | solution.py:108
  976.4 79.2 %collective-permute-start.196 = (bf16[216,1536]{1,0:T(8,128)(2,1)S(1)}, bf16[216,1536]{1,0:T(8,128)(2,1)S(1)}, u32[]{:S(2)}, u32[]{:S(2)}) collective-permute-start(bf16[216,1536]{1,0:T(8,128)(2,1)S(1)} %get-tuple-element.124), channel_id=1, source_target_pairs={{0,24},{4,28},{8,0},{12,4},{16,8},{20,12},{24,16},{28,20},{1,25},{... | collective-permute-start | bytes 1990664 | tf_op jit(solution)/shard_map/ppermute | solution.py:220
  986.7 72.7 %collective-permute-start.185 = (bf16[192,1728]{1,0:T(8,128)(2,1)S(1)}, bf16[192,1728]{1,0:T(8,128)(2,1)S(1)}, u32[]{:S(2)}, u32[]{:S(2)}) collective-permute-start(bf16[192,1728]{1,0:T(8,128)(2,1)S(1)} %get-tuple-element.95), channel_id=1, source_target_pairs={{0,8},{4,12},{8,16},{12,20},{16,24},{20,28},{24,0},{28,4},{1,9},{5... | collective-permute-start | bytes 1990664 | tf_op jit(solution)/shard_map/ppermute | solution.py:220
  988.3 114.2 %collective-permute-start.187 = (bf16[192,1728]{1,0:T(8,128)(2,1)S(1)}, bf16[192,1728]{1,0:T(8,128)(2,1)S(1)}, u32[]{:S(2)}, u32[]{:S(2)}) collective-permute-start(bf16[192,1728]{1,0:T(8,128)(2,1)S(1)} %get-tuple-element.97), channel_id=1, source_target_pairs={{0,16},{4,20},{8,24},{12,28},{16,0},{20,4},{24,8},{28,12},{1,17},{... | collective-permute-start | bytes 1990664 | tf_op jit(solution)/shard_map/ppermute | solution.py:220
  1016.8 85.8 %collective-permute-start.189 = (bf16[192,1728]{1,0:T(8,128)(2,1)S(1)}, bf16[192,1728]{1,0:T(8,128)(2,1)S(1)}, u32[]{:S(2)}, u32[]{:S(2)}) collective-permute-start(bf16[192,1728]{1,0:T(8,128)(2,1)S(1)} %get-tuple-element.96), channel_id=1, source_target_pairs={{0,24},{4,28},{8,0},{12,4},{16,8},{20,12},{24,16},{28,20},{1,25},{... | collective-permute-start | bytes 1990664 | tf_op jit(solution)/shard_map/ppermute | solution.py:220
  1058.9 81.5 %collective-permute-start.183 = (bf16[192,1728]{1,0:T(8,128)(2,1)}, bf16[192,1728]{1,0:T(8,128)(2,1)}, u32[]{:S(2)}, u32[]{:S(2)}) collective-permute-start(bf16[192,1728]{1,0:T(8,128)(2,1)} %get-tuple-element.106), channel_id=1, source_target_pairs={{0,4},{4,0},{8,12},{12,8},{16,20},{20,16},{24,28},{28,24},{1,5},{5... | collective-permute-start | bytes 1990664 | tf_op jit(solution)/shard_map/ppermute | solution.py:108
  1059.5 81.0 %collective-permute-start.178 = (bf16[192,1728]{1,0:T(8,128)(2,1)}, bf16[192,1728]{1,0:T(8,128)(2,1)}, u32[]{:S(2)}, u32[]{:S(2)}) collective-permute-start(bf16[192,1728]{1,0:T(8,128)(2,1)} %get-tuple-element.102), channel_id=1, source_target_pairs={{0,8},{4,12},{8,16},{12,20},{16,24},{20,28},{24,0},{28,4},{1,9},{5... | collective-permute-start | bytes 1990664 | tf_op jit(solution)/shard_map/ppermute | solution.py:220
  1302.9 67.3 %collective-permute-start.142 = (bf16[192,1728]{1,0:T(8,128)(2,1)S(1)}, bf16[192,1728]{1,0:T(8,128)(2,1)S(1)}, u32[]{:S(2)}, u32[]{:S(2)}) collective-permute-start(bf16[192,1728]{1,0:T(8,128)(2,1)S(1)} %get-tuple-element.119), channel_id=1, source_target_pairs={{0,4},{4,0},{8,12},{12,8},{16,20},{20,16},{24,28},{28,24},{1,5},{5... | collective-permute-start | bytes 1990664 | tf_op jit(solution)/shard_map/ppermute | solution.py:108
  1312.4 72.6 %collective-permute-start.144 = (bf16[192,1728]{1,0:T(8,128)(2,1)S(1)}, bf16[192,1728]{1,0:T(8,128)(2,1)S(1)}, u32[]{:S(2)}, u32[]{:S(2)}) collective-permute-start(bf16[192,1728]{1,0:T(8,128)(2,1)S(1)} %get-tuple-element.122), channel_id=1, source_target_pairs={{0,4},{4,0},{8,12},{12,8},{16,20},{20,16},{24,28},{28,24},{1,5},{5... | collective-permute-start | bytes 1990664 | tf_op jit(solution)/shard_map/ppermute | solution.py:108
  1327.2 72.6 %collective-permute-start.146 = (bf16[192,1728]{1,0:T(8,128)(2,1)S(1)}, bf16[192,1728]{1,0:T(8,128)(2,1)S(1)}, u32[]{:S(2)}, u32[]{:S(2)}) collective-permute-start(bf16[192,1728]{1,0:T(8,128)(2,1)S(1)} %get-tuple-element.121), channel_id=1, source_target_pairs={{0,4},{4,0},{8,12},{12,8},{16,20},{20,16},{24,28},{28,24},{1,5},{5... | collective-permute-start | bytes 1990664 | tf_op jit(solution)/shard_map/ppermute | solution.py:108
  1341.3 67.3 %collective-permute-start.119 = (bf16[160,1536]{1,0:T(8,128)(2,1)S(1)}, bf16[160,1536]{1,0:T(8,128)(2,1)S(1)}, u32[]{:S(2)}, u32[]{:S(2)}) collective-permute-start(bf16[160,1536]{1,0:T(8,128)(2,1)S(1)} %copy-done.101), channel_id=1, source_target_pairs={{0,1},{1,0},{2,3},{3,2},{4,5},{5,4},{6,7},{7,6},{8,9},{9,8},{10,11... | collective-permute-start | bytes 1474568 | tf_op jit(solution)/shard_map/ppermute | solution.py:108
  1355.5 58.5 %collective-permute-start.162 = (bf16[216,1536]{1,0:T(8,128)(2,1)S(1)}, bf16[216,1536]{1,0:T(8,128)(2,1)S(1)}, u32[]{:S(2)}, u32[]{:S(2)}) collective-permute-start(bf16[216,1536]{1,0:T(8,128)(2,1)S(1)} %copy-done.77), channel_id=1, source_target_pairs={{0,4},{4,0},{8,12},{12,8},{16,20},{20,16},{24,28},{28,24},{1,5},{5... | collective-permute-start | bytes 1990664 | tf_op jit(solution)/shard_map/ppermute | solution.py:108
  1370.3 57.7 %collective-permute-start.155 = (bf16[192,1728]{1,0:T(8,128)(2,1)S(1)}, bf16[192,1728]{1,0:T(8,128)(2,1)S(1)}, u32[]{:S(2)}, u32[]{:S(2)}) collective-permute-start(bf16[192,1728]{1,0:T(8,128)(2,1)S(1)} %get-tuple-element.113), channel_id=1, source_target_pairs={{0,4},{4,0},{8,12},{12,8},{16,20},{20,16},{24,28},{28,24},{1,5},{5... | collective-permute-start | bytes 1990664 | tf_op jit(solution)/shard_map/ppermute | solution.py:108
  1414.0 81.4 %collective-permute-start.150 = (bf16[192,1728]{1,0:T(8,128)(2,1)S(1)}, bf16[192,1728]{1,0:T(8,128)(2,1)S(1)}, u32[]{:S(2)}, u32[]{:S(2)}) collective-permute-start(bf16[192,1728]{1,0:T(8,128)(2,1)S(1)} %get-tuple-element.109), channel_id=1, source_target_pairs={{0,8},{4,12},{8,16},{12,20},{16,24},{20,28},{24,0},{28,4},{1,9},{5... | collective-permute-start | bytes 1990664 | tf_op jit(solution)/shard_map/ppermute | solution.py:220
  1428.0 109.5 %collective-permute-start.152 = (bf16[192,1728]{1,0:T(8,128)(2,1)S(1)}, bf16[192,1728]{1,0:T(8,128)(2,1)S(1)}, u32[]{:S(2)}, u32[]{:S(2)}) collective-permute-start(bf16[192,1728]{1,0:T(8,128)(2,1)S(1)} %get-tuple-element.111), channel_id=1, source_target_pairs={{0,16},{4,20},{8,24},{12,28},{16,0},{20,4},{24,8},{28,12},{1,17},{... | collective-permute-start | bytes 1990664 | tf_op jit(solution)/shard_map/ppermute | solution.py:220
  1432.7 109.3 %collective-permute-start.154 = (bf16[192,1728]{1,0:T(8,128)(2,1)}, bf16[192,1728]{1,0:T(8,128)(2,1)}, u32[]{:S(2)}, u32[]{:S(2)}) collective-permute-start(bf16[192,1728]{1,0:T(8,128)(2,1)} %get-tuple-element.110), channel_id=1, source_target_pairs={{0,24},{4,28},{8,0},{12,4},{16,8},{20,12},{24,16},{28,20},{1,25},{... | collective-permute-start | bytes 1990664 | tf_op jit(solution)/shard_map/ppermute | solution.py:220
  1451.6 95.5 %collective-permute-start.148 = (bf16[192,1728]{1,0:T(8,128)(2,1)}, bf16[192,1728]{1,0:T(8,128)(2,1)S(1)}, u32[]{:S(2)}, u32[]{:S(2)}) collective-permute-start(bf16[192,1728]{1,0:T(8,128)(2,1)} %get-tuple-element.120), channel_id=1, source_target_pairs={{0,4},{4,0},{8,12},{12,8},{16,20},{20,16},{24,28},{28,24},{1,5},{5... | collective-permute-start | bytes 1990664 | tf_op jit(solution)/shard_map/ppermute | solution.py:108
  1453.1 99.9 %collective-permute-start.143 = (bf16[192,1728]{1,0:T(8,128)(2,1)}, bf16[192,1728]{1,0:T(8,128)(2,1)}, u32[]{:S(2)}, u32[]{:S(2)}) collective-permute-start(bf16[192,1728]{1,0:T(8,128)(2,1)} %get-tuple-element.116), channel_id=1, source_target_pairs={{0,8},{4,12},{8,16},{12,20},{16,24},{20,28},{24,0},{28,4},{1,9},{5... | collective-permute-start | bytes 1990664 | tf_op jit(solution)/shard_map/ppermute | solution.py:220
  1495.4 71.7 %collective-permute-start.145 = (bf16[192,1728]{1,0:T(8,128)(2,1)}, bf16[192,1728]{1,0:T(8,128)(2,1)}, u32[]{:S(2)}, u32[]{:S(2)}) collective-permute-start(bf16[192,1728]{1,0:T(8,128)(2,1)} %get-tuple-element.118), channel_id=1, source_target_pairs={{0,16},{4,20},{8,24},{12,28},{16,0},{20,4},{24,8},{28,12},{1,17},{... | collective-permute-start | bytes 1990664 | tf_op jit(solution)/shard_map/ppermute | solution.py:220
  1593.3 70.7 %collective-permute-start.126 = (bf16[160,1536]{1,0:T(8,128)(2,1)}, bf16[160,1536]{1,0:T(8,128)(2,1)}, u32[]{:S(2)}, u32[]{:S(2)}) collective-permute-start(bf16[160,1536]{1,0:T(8,128)(2,1)} %get-tuple-element.169), channel_id=1, source_target_pairs={{0,1},{1,0},{2,3},{3,2},{4,5},{5,4},{6,7},{7,6},{8,9},{9,8},{10,11... | collective-permute-start | bytes 1474568 | tf_op jit(solution)/shard_map/ppermute | solution.py:108
  1625.2 80.8 %collective-permute-start.125 = (bf16[160,1536]{1,0:T(8,128)(2,1)}, bf16[160,1536]{1,0:T(8,128)(2,1)}, u32[]{:S(2)}, u32[]{:S(2)}) collective-permute-start(bf16[160,1536]{1,0:T(8,128)(2,1)} %get-tuple-element.168), channel_id=1, source_target_pairs={{0,1},{1,0},{2,3},{3,2},{4,5},{5,4},{6,7},{7,6},{8,9},{9,8},{10,11... | collective-permute-start | bytes 1474568 | tf_op jit(solution)/shard_map/ppermute | solution.py:108
  (370 other events, 10838.3 us)

commit v2 on v1

--- a/solution.py
+++ b/solution.py
@@ -134,16 +134,16 @@
     return jnp.stack([own ^ bit for bit in TENSOR_ORDER]) if count == 4 else jnp.arange(count)
 
 
-def gather_sum(lhs_rows, rhs_matrix, send_type=jnp.float32):
-    return scatter_rows(dot_rows(lhs_rows, rhs_matrix).astype(send_type))
-
-
-def sum_input_grads(grad_pairs):
+def gather_sum(lhs_rows, rhs_matrix):
+    return scatter_rows(dot_rows(lhs_rows, rhs_matrix))
+
+
+def sum_input_grads(grad_pairs, scatter):
     running = None
     for grad_block, weight in grad_pairs:
         product_part = dot_last(grad_block, weight)
         running = product_part if running is None else running + product_part
-    return scatter_rows(running.astype(jnp.bfloat16))
+    return scatter(running.astype(jnp.bfloat16))
 
 
 def flip_slots(slots, own):
@@ -178,61 +178,179 @@
     return values
 
 
-def shift_pairs(step):
-    return [(z * 2 + y, (z + step) % 4 * 2 + y) for z in range(4) for y in range(2)]
-
-
-def fetch_matrix(piece):
-    if lax.axis_size("dp") != 8:
-        whole = lax.all_gather(piece, "dp", axis=0, tiled=True)
-        return whole, ()
-    own = lax.axis_index("dp")
-    z_own, y_own = own // 2, own % 2
-    column = [piece] + [lax.ppermute(piece, "dp", shift_pairs(step)) for step in (1, 2, 3)]
-    whole = jnp.zeros((8,) + piece.shape, piece.dtype)
-    for step in range(4):
-        slot = (z_own + 4 - step) % 4 * 2
-        whole = lax.dynamic_update_index_in_dim(whole, column[step], slot + y_own, 0)
-        other = swap(column[step], "dp", 1)
-        whole = lax.dynamic_update_index_in_dim(whole, other, slot + 1 - y_own, 0)
-    return whole.reshape((-1,) + piece.shape[1:]), tuple(column[1:])
-
-
-def reduce_matrix(grad):
-    dp_count = lax.axis_size("dp")
-    if dp_count != 8:
+def is_grid():
+    return lax.axis_size("dp") == 8 and lax.axis_size("tensor") == 4
+
+
+def dp_bit(bit):
+    return (lax.axis_index("dp") // bit) % 2
+
+
+def pair_up(own, other, bit, axis=0):
+    shape = [1] * (own.ndim + 1)
+    shape[axis] = 2
+    place = lax.broadcasted_iota(jnp.int32, tuple(shape), axis)
+    return jnp.where(
+        place == dp_bit(bit), jnp.expand_dims(own, axis), jnp.expand_dims(other, axis)
+    )
+
+
+def pick(values, bit, axis, same):
+    side = dp_bit(bit) if same else 1 - dp_bit(bit)
+    return lax.dynamic_index_in_dim(values, side, axis, keepdims=False)
+
+
+class Links:
+    def __init__(self, depth=2):
+        self.depth = depth
+        self.past = {1: [], 2: []}
+
+    def send(self, values, bit):
+        past = self.past[1 if bit == 1 else 2]
+        if len(past) >= self.depth:
+            values, _ = lax.optimization_barrier((values, past[-self.depth]))
+        got = swap(values, "dp", bit)
+        past.append(got)
+        return got
+
+
+class Fetch:
+    def __init__(self, links, piece, kind):
+        self.links, self.kind = links, kind
+        self.rows, self.cols = piece.shape
+        self.piece = piece
+
+    def near(self):
+        piece = self.piece
+        if self.kind == "half":
+            view = piece.reshape(self.rows, 2, 2, self.cols // 4)
+            own = pick(view, 2, 2, True).reshape(self.rows, -1)
+            away = pick(view, 2, 2, False).reshape(self.rows, -1)
+        else:
+            own = away = piece
+        self.held = pair_up(own, self.links.send(away, 2), 2)
+
+    def far(self):
+        held = self.piece if self.kind == "rows" else self.held
+        self.held = pair_up(held, self.links.send(held, 4), 4)
+
+    def side(self):
+        held = self.held
+        whole = pair_up(held, self.links.send(held, 1), 1, axis=held.ndim - 2)
+        self.whole = whole.reshape(-1, whole.shape[-1])
+
+
+class Reduce:
+    def __init__(self, links, grad, kind):
+        self.links, self.kind = links, kind
+        lead = (2, 2) if kind == "rows" else (2, 2, 2)
+        rows = grad.shape[0] // math.prod(lead)
+        self.held = grad.astype(jnp.bfloat16).reshape(lead + (rows, grad.shape[1]))
+
+    def step(self, bit, axis):
+        got = self.links.send(pick(self.held, bit, axis, False), bit)
+        kept = pick(self.held, bit, axis, True)
+        return kept.astype(jnp.float32) + got.astype(jnp.float32)
+
+    def side(self):
+        self.held = self.step(1, self.held.ndim - 3).astype(jnp.bfloat16)
+
+    def far(self):
+        total = self.step(4, 0)
+        self.held = total if self.kind == "rows" else total.astype(jnp.bfloat16)
+
+    def near(self):
+        held = self.held
+        if self.kind == "whole":
+            self.held = self.step(2, 0)
+        elif self.kind == "half":
+            got = self.links.send(pick(held, 2, 0, False), 2)
+            kept = pick(held, 2, 0, True)
+            rows, cols = kept.shape
+            both = pair_up(
+                kept.reshape(rows, 2, cols // 2), got.reshape(rows, 2, cols // 2), 2, axis=2
+            )
+            self.held = both.reshape(rows, -1).astype(jnp.float32)
+
+
+def gather_group(values):
+    if not is_grid():
+        return gather_rows(values)
+    half = values.shape[0] // 2
+    x_rows = swap(values, "tensor", 2)
+    z_rows = swap(values, "dp", 2)
+    cross_top = swap(z_rows[:half], "tensor", 2)
+    cross_low = swap(x_rows[half:], "dp", 2)
+    first = jnp.concatenate([values, x_rows, z_rows], axis=0)
+    cross = jnp.concatenate([cross_top, cross_low], axis=0)
+    return jnp.concatenate(
+        [first, swap(first, "tensor", 1), cross, swap(cross, "tensor", 1)], axis=0
+    )
+
+
+def scatter_group(partial):
+    if not is_grid():
+        return scatter_rows(partial)
+    kind = partial.dtype
+    rows = partial.shape[0] // 8
+    half = rows // 2
+    wide = partial.astype(jnp.float32)
+    cross_in = swap(partial[7 * rows :], "tensor", 1)
+    first_in = swap(partial[3 * rows : 6 * rows], "tensor", 1)
+    cross = wide[6 * rows : 7 * rows] + cross_in.astype(jnp.float32)
+    top_in = swap(cross[:half].astype(kind), "tensor", 2)
+    low_in = swap(cross[half:].astype(kind), "dp", 2)
+    first = wide[: 3 * rows] + first_in.astype(jnp.float32)
+    x_sum = jnp.concatenate(
+        [first[rows : rows + half], first[rows + half : 2 * rows] + low_in.astype(jnp.float32)],
+        axis=0,
+    )
+    z_sum = jnp.concatenate(
+        [first[2 * rows : 2 * rows + half] + top_in.astype(jnp.float32), first[2 * rows + half :]],
+        axis=0,
+    )
+    x_in = swap(x_sum.astype(kind), "tensor", 2)
+    z_in = swap(z_sum.astype(kind), "dp", 2)
+    return first[:rows] + x_in.astype(jnp.float32) + z_in.astype(jnp.float32)
+
+
+def fetch_all(pieces, kinds):
+    if not is_grid():
+        return [lax.all_gather(piece, "dp", axis=0, tiled=True) for piece in pieces]
+    links = Links()
+    items = [Fetch(links, piece, kind) for piece, kind in zip(pieces, kinds)]
+    w_in, w_out, gate_1, up_1, down_1, w_qkv, w_attn, gate_2, up_2, down_2 = items
+    w_in.near()
+    w_in.far()
+    gate_1.near()
+    up_1.near()
+    w_in.side()
+    w_out.near()
+    w_out.far()
+    gate_1.far()
+    w_out.side()
+    gate_1.side()
+    for before, after in (
+        (gate_1, up_1), (up_1, down_1), (down_1, w_qkv), (w_qkv, w_attn),
+        (w_attn, gate_2), (gate_2, up_2), (up_2, down_2),
+    ):
+        if after in (w_qkv, w_attn, gate_2):
+            after.near()
+        if after is gate_2:
+            up_2.near()
+        after.far()
+        after.side()
+    return [item.whole for item in items]
+
+
+def reduce_matrix(grad, kind, links):
+    if not is_grid():
         return lax.psum_scatter(grad.astype(jnp.float32), "dp", scatter_dimension=0, tiled=True)
-    own = lax.axis_index("dp")
-    z_own, y_own = own // 2, own % 2
-    blocks = grad.astype(jnp.bfloat16).reshape((4, 2, grad.shape[0] // 8, grad.shape[1]))
-
-    def block(slot, side):
-        return lax.dynamic_slice(
-            blocks, (slot, side, 0, 0), (1, 1) + blocks.shape[2:]
-        ).reshape(blocks.shape[2:])
-
-    total = None
-    for step in (1, 2, 3, 0):
-        slot = (z_own + step) % 4
-        other = swap(block(slot, 1 - y_own), "dp", 1)
-        pair = block(slot, y_own).astype(jnp.float32) + other.astype(jnp.float32)
-        if step:
-            pair = lax.ppermute(pair.astype(jnp.bfloat16), "dp", shift_pairs(step))
-            pair = pair.astype(jnp.float32)
-        total = pair if total is None else total + pair
-    return total
-
-
-def fetch_all(pieces):
-    result = []
-    landed = []
-    for number, piece in enumerate(pieces):
-        if number >= 2 and landed[number - 2]:
-            piece, _ = lax.optimization_barrier((piece, landed[number - 2]))
-        whole, hops = fetch_matrix(piece)
-        landed.append(hops)
-        result.append(whole)
-    return result
+    item = Reduce(links, grad, kind)
+    item.side()
+    item.far()
+    item.near()
+    return item.held
 
 
 class FlatPlan:
@@ -287,10 +405,10 @@
 
     def body(cur_ref, next_ref, out_ref, work_ref):
         cur = cur_ref[0, 0].reshape(rows, 128)
-        work_ref[0:rows, :] = cur
-        work_ref[rows : rows + 8, :] = next_ref[0, 0].reshape(8, 128)
-        low = pltpu.roll(work_ref[skip : skip + rows, :], 128 - lanes, 1)
-        high = pltpu.roll(work_ref[skip + 1 : skip + 1 + rows, :], 128 - lanes, 1)
+        work_ref[0:rows, :] = pltpu.roll(cur, 128 - lanes, 1)
+        work_ref[rows : rows + 8, :] = pltpu.roll(next_ref[0, 0].reshape(8, 128), 128 - lanes, 1)
+        low = work_ref[skip : skip + rows, :]
+        high = work_ref[skip + 1 : skip + 1 + rows, :]
         moved = jnp.where(lane_ids(rows) < 128 - lanes, low, high)
         front = pl.program_id(0) < plan.front_blocks
         out_ref[...] = jnp.where(front, cur, moved).astype(jnp.bfloat16)
@@ -457,10 +575,11 @@
     return (residual + gather_sum(conv_out, w_out), kept_vals)
 
 
-def mixer_backward(grad_out, residual, gain_vec, weights, kept_vals, owners):
+def mixer_backward(grad_out, residual, gain_vec, weights, kept_vals, owners, links):
     w_in, kernel, w_out = weights
     normed_rows, gate_b, gate_c, values, padded, conv_mixed, conv_out = kept_vals
     grad_rows = gather_rows(grad_out.astype(jnp.bfloat16))
+    grad_out_w = grad_product(conv_out, grad_rows, "whole", links)
     d_conv = dot_last(grad_rows, w_out).reshape(conv_mixed.shape)
     d_gate_c = d_conv * conv_mixed
     d_mixed = d_conv * gate_c
@@ -485,38 +604,40 @@
         ],
         axis=-1,
     ).reshape(normed_rows.shape[0], -1)
-    d_normed = sum_input_grads(((d_proj, w_in),))
+    d_normed = sum_input_grads(((d_proj, w_in),), scatter_rows)
     d_resid, d_gain = norm_back(residual, gain_vec, d_normed)
-    grads = (grad_product(normed_rows, d_proj), grad_product(conv_out, grad_rows))
+    grads = (grad_product(normed_rows, d_proj, "whole", links), grad_out_w)
     return (grad_out + d_resid, d_gain, d_kernel, grads)
 
 
-def grad_product(lhs_rows, rhs_rows):
-    return reduce_matrix(dot_first(lhs_rows, rhs_rows).astype(jnp.bfloat16))
+def grad_product(lhs_rows, rhs_rows, kind, links):
+    return reduce_matrix(dot_first(lhs_rows, rhs_rows).astype(jnp.bfloat16), kind, links)
 
 
 def ffn_forward(residual, gain_vec, weights, send_type=jnp.float32):
     w_gate, w_up, w_down = weights
-    normed_rows = gather_rows(rms_norm(residual, gain_vec).astype(jnp.bfloat16))
+    normed_rows = gather_group(rms_norm(residual, gain_vec).astype(jnp.bfloat16))
     gate_vals = dot_rows(normed_rows, w_gate)
     up_vals = dot_rows(normed_rows, w_up)
     hidden = gated_unit(gate_vals, up_vals).astype(jnp.bfloat16)
-    return (residual + gather_sum(hidden, w_down, send_type), (normed_rows, gate_vals, up_vals, hidden))
-
-
-def ffn_backward(grad_out, residual, gain_vec, weights, kept_vals):
+    branch = scatter_group(dot_rows(hidden, w_down).astype(send_type))
+    return (residual + branch, (normed_rows, gate_vals, up_vals, hidden))
+
+
+def ffn_backward(grad_out, residual, gain_vec, weights, kept_vals, links):
     w_gate, w_up, w_down = weights
     normed_rows, gate_vals, up_vals, hidden = kept_vals
-    grad_rows = gather_rows(grad_out.astype(jnp.bfloat16))
-    grad_down = grad_product(hidden, grad_rows)
+    grad_rows = gather_group(grad_out.astype(jnp.bfloat16))
+    grad_down = grad_product(hidden, grad_rows, "rows", links)
     d_hidden = dot_last(grad_rows, w_down)
     primal_out, pullback = jax.vjp(gated_unit, gate_vals, up_vals)
     d_gate, d_up = pullback(d_hidden)
     d_gate = d_gate.astype(jnp.bfloat16)
     d_up = d_up.astype(jnp.bfloat16)
-    d_normed = sum_input_grads(((d_gate, w_gate), (d_up, w_up)))
+    d_normed = sum_input_grads(((d_gate, w_gate), (d_up, w_up)), scatter_group)
     d_resid, d_gain = norm_back(residual, gain_vec, d_normed)
-    grads = (grad_product(normed_rows, d_gate), grad_product(normed_rows, d_up), grad_down)
+    grad_gate = grad_product(normed_rows, d_gate, "half", links)
+    grads = (grad_gate, grad_product(normed_rows, d_up, "half", links), grad_down)
     return (grad_out + d_resid, d_gain, grads)
 
 
@@ -569,14 +690,14 @@
 
 
 def attention_backward(
-    grad_out, residual, gain_vec, gain_query, gain_key, weights, tables, causal, kept_vals
+    grad_out, residual, gain_vec, gain_query, gain_key, weights, tables, causal, kept_vals, links
 ):
     w_qkv, w_attn = weights
     cosines, sines = tables
     normed_rows, query_raw, key_raw, query_b, key_b, value_b, log_sum, attended = kept_vals
     seq_len = normed_rows.shape[0]
     grad_rows = gather_rows(grad_out.astype(jnp.bfloat16))
-    grad_attn = grad_product(attended, grad_rows)
+    grad_attn = grad_product(attended, grad_rows, "whole", links)
     d_attended = dot_last(grad_rows, w_attn).astype(jnp.bfloat16).reshape(query_b.shape)
     soft_probs = jnp.exp(score_block(query_b, key_b, causal) - log_sum)
     d_probs = jnp.einsum("snge,tne->ngst", d_attended, value_b, preferred_element_type=jnp.float32)
@@ -617,9 +738,9 @@
         ],
         axis=1,
     )
-    d_normed = sum_input_grads(((d_qkv, w_qkv),))
+    d_normed = sum_input_grads(((d_qkv, w_qkv),), scatter_rows)
     d_resid, d_gain = norm_back(residual, gain_vec, d_normed)
-    grads = (grad_product(normed_rows, d_qkv), grad_attn)
+    grads = (grad_product(normed_rows, d_qkv, "whole", links), grad_attn)
     return (grad_out + d_resid, d_gain, d_gain_query, d_gain_key, grads)
 
 
@@ -668,8 +789,10 @@
     gain_key = gain_vector[4 * MODEL_DIM + HEAD_DIM : 4 * MODEL_DIM + 2 * HEAD_DIM]
 
     w_in, w_out, gate_1, up_1, down_1, w_qkv, w_attn, gate_2, up_2, down_2 = fetch_all(
-        [pieces[0], pieces[2], *pieces[3:6], qkv_piece, pieces[9], *pieces[10:13]]
-    )
+        [pieces[0], pieces[2], *pieces[3:6], qkv_piece, pieces[9], *pieces[10:13]],
+        ["whole", "whole", "half", "half", "rows", "whole", "whole", "half", "half", "rows"],
+    )
+    links = Links()
 
     rows_dev = tokens.shape[0]
     positions = (owners[:, None] * rows_dev + jnp.arange(rows_dev)[None, :]).reshape(-1)
@@ -692,7 +815,7 @@
 
     grad_four = cotangent.astype(jnp.float32)
     grad_three, d_gain_four, grads_ffn_two = ffn_backward(
-        grad_four, resid_three, gain_four, ffn_two, kept_ffn_two
+        grad_four, resid_three, gain_four, ffn_two, kept_ffn_two, links
     )
     grad_two, d_gain_three, d_gain_query, d_gain_key, grads_attn = attention_backward(
         grad_three,
@@ -704,12 +827,13 @@
         tables,
         causal,
         kept_attn,
+        links,
     )
     grad_one, d_gain_two, grads_ffn_one = ffn_backward(
-        grad_two, resid_one, gain_two, ffn_one, kept_ffn_one
+        grad_two, resid_one, gain_two, ffn_one, kept_ffn_one, links
     )
     grad_zero, d_gain_one, d_kernel, grads_mix = mixer_backward(
-        grad_one, resid_zero, gain_one, mix_weights, kept_mix, owners
+        grad_one, resid_zero, gain_one, mix_weights, kept_mix, owners, links
     )
 
     gain_partial = jnp.concatenate(

time: 1850 us -> 1500 us (0.81)
  starting transfers between devices: 497 us -> 145 us
  other arithmetic: 83.7 us -> 131 us
  waiting for transfers between devices: 789 us -> 760 us
  matrix products: 179 us -> 155 us
    ppermute x60 -> x0, starting transfers between devices: 353 us -> none  [the longest x30 232 us: reduce_matrix(): pair = lax.ppermute(pair.astype(jnp.bfloat16), 'dp', shift_pairs(step))]
    ppermute x60 -> x0, waiting for transfers between devices: 309 us -> none  [the longest x30 172 us: fetch_matrix(): lax.ppermute(piece, 'dp', shift_pairs(step))]
    ppermute x158, waiting for transfers between devices: 480 us -> 760 us  [swap(): return lax.ppermute(values, axis_name, [(i, i ^ bit) for i in range(count)])]
    broadcast_in_dim x4 -> x43, local copies, waits for them, and re-layouts: 3.05 us -> 56.8 us  [pair_up(): jnp.where(place == dp_bit(bit), jnp.expand_dims(own, axis), jnp.expand_di...]
    dynamic_update_slice x80 -> x0, local copies, waits for them, and re-layouts: 48.6 us -> none  [the longest x40 28.7 us: fetch_matrix(): lax.dynamic_update_index_in_dim(whole, column[step], slot + y_own, 0)]
    select_n x0 -> x17, other arithmetic: none -> 31.8 us  [pair_up(): jnp.where(place == dp_bit(bit), jnp.expand_dims(own, axis), jnp.expand_di...]
    dynamic_slice x0 -> x6, local copies, waits for them, and re-layouts: none -> 26.8 us  [pick(): return lax.dynamic_index_in_dim(values, side, axis, keepdims=False)]
  transfers between devices with their start and end apart: 218 -> 158, of which waited for: 86 -> 67; matrix products, arithmetic and copies ran while one was open for 19% -> 25% of each run, Pallas kernels for 1% -> 1%
where the time goes in v2:
time: 1500 us; the launch traced here: 1490 us
  waiting for transfers between devices  760 us (51%)
  local copies, waits for them, and re-layouts  198 us (13%)
  matrix products  155 us (10%)
  starting transfers between devices  145 us (10%)
  other arithmetic  131 us (9%)
  Pallas kernels  94 us (6%)
    ppermute x158, waiting for transfers between devices, swap(): return lax.ppermute(values, axis_name, [(i, i ^ bit) for i in range(count)])  760 us
    ppermute x158, starting transfers between devices, swap(): return lax.ppermute(values, axis_name, [(i, i ^ bit) for i in range(count)])  145 us
    broadcast_in_dim x43, local copies, waits for them, and re-layouts, pair_up(): jnp.where(place == dp_bit(bit), jnp.expand_dims(own, axis), jnp.expand_di...  56.8 us
    dot_general x10, matrix products, dot_rows(): return jnp.dot(lhs_rows, rhs_matrix, preferred_element_type=jnp.float32)  48.3 us
    dot_general x10, matrix products, dot_first(): lax.dot_general(lhs_rows, rhs_rows, (((0,), (0,)), ((), ())), preferred_e...  46.6 us
    dot_general x10, matrix products, dot_last(): lax.dot_general(lhs_rows, rhs_matrix, (((1,), (1,)), ((), ())), preferred...  43.3 us
    pallas_call x1, Pallas kernels, moments_pass(): pl.pallas_call(body, name='moments_pass', grid_spec=pltpu.PrefetchScalarG...  39.7 us
    pallas_call x1, Pallas kernels, weights_pass(): pl.pallas_call(body, name='weights_pass', grid_spec=pltpu.PrefetchScalarG...  32.1 us
  transfers between devices with their start and end apart: 158, of which 67 were waited for; matrix products, arithmetic and copies ran while one was open for 25% of the time, Pallas kernels for 1%

profile of v2, /device:TPU:0, one launch (start us, length us, event | category | flops | bytes accessed | tf_op | source)
XLA Modules:
  0.0 1487.3 jit_solution(3990487850403982777)
XLA Ops:
  9.1 22.1 %to_rows.1 = bf16[19584,128]{1,0:T(8,128)(2,1)} custom-call(f32[1,1,2482320]{2,1,0:T(1,128)} %w_ref.3, f32[1,1,2482320]{2,1,0:T(1,128)} %w_ref.3), custom_call_target="tpu_custom_call" | custom-call | flops 2482320 | bytes 14893920 | tf_op jit(solution)/shard_map/to_rows/pallas_call | solution.py:416
  46.4 11.5 dynamic-slice_reduce_fusion.4
  68.3 12.0 dynamic-slice_reduce_fusion.1
  89.4 10.0 collective-permute-done.3
  125.0 25.6 %collective-permute-done.19 = bf16[2,48,1536]{2,1,0:T(8,128)(2,1)S(1)} collective-permute-done((bf16[2,48,1536]{2,1,0:T(8,128)(2,1)S(1)}, bf16[2,48,1536]{2,1,0:T(8,128)(2,1)S(1)}, u32[]{:S(2)}, u32[]{:S(2)}) %collective-permute-start.19) | collective-permute-done | bytes 294944 | tf_op jit(solution)/shard_map/ppermute | solution.py:108
  162.5 17.7 %collective-permute-done.30 = bf16[2,192,864]{2,1,0:T(8,128)(2,1)} collective-permute-done((bf16[2,192,864]{2,1,0:T(8,128)(2,1)S(1)}, bf16[2,192,864]{2,1,0:T(8,128)(2,1)}, u32[]{:S(2)}, u32[]{:S(2)}) %collective-permute-start.30) | collective-permute-done | bytes 663584 | tf_op jit(solution)/shard_map/ppermute | solution.py:108
  180.2 29.0 %collective-permute-done.32 = bf16[2,192,864]{2,1,0:T(8,128)(2,1)} collective-permute-done((bf16[2,192,864]{2,1,0:T(8,128)(2,1)S(1)}, bf16[2,192,864]{2,1,0:T(8,128)(2,1)}, u32[]{:S(2)}, u32[]{:S(2)}) %collective-permute-start.32) | collective-permute-done | bytes 663584 | tf_op jit(solution)/shard_map/ppermute | solution.py:108
  209.4 19.2 %collective-permute-done.45 = bf16[192,640]{1,0:T(8,128)(2,1)} collective-permute-done((bf16[192,640]{1,0:T(8,128)(2,1)}, bf16[192,640]{1,0:T(8,128)(2,1)}, u32[]{:S(2)}, u32[]{:S(2)}) %collective-permute-start.45) | collective-permute-done | bytes 245792 | tf_op jit(solution)/shard_map/ppermute | solution.py:108
  236.8 17.7 %collective-permute-done.46 = bf16[2,192,640]{2,1,0:T(8,128)(2,1)S(1)} collective-permute-done((bf16[2,192,640]{2,1,0:T(8,128)(2,1)S(1)}, bf16[2,192,640]{2,1,0:T(8,128)(2,1)S(1)}, u32[]{:S(2)}, u32[]{:S(2)}) %collective-permute-start.46) | collective-permute-done | bytes 491552 | tf_op jit(solution)/shard_map/ppermute | solution.py:108
  259.6 9.1 collective-permute-done.49
  290.8 53.9 %collective-permute-done.61 = bf16[2,192,864]{2,1,0:T(8,128)(2,1)} collective-permute-done((bf16[2,192,864]{2,1,0:T(8,128)(2,1)}, bf16[2,192,864]{2,1,0:T(8,128)(2,1)}, u32[]{:S(2)}, u32[]{:S(2)}) %collective-permute-start.61) | collective-permute-done | bytes 663584 | tf_op jit(solution)/shard_map/ppermute | solution.py:108
  352.1 23.6 %collective-permute-done.66 = bf16[216,1536]{1,0:T(8,128)(2,1)S(1)} collective-permute-done((bf16[216,1536]{1,0:T(8,128)(2,1)S(1)}, bf16[216,1536]{1,0:T(8,128)(2,1)S(1)}, u32[]{:S(2)}, u32[]{:S(2)}) %collective-permute-start.66) | collective-permute-done | bytes 663584 | tf_op jit(solution)/shard_map/ppermute | solution.py:108
  387.8 24.9 %collective-permute-done.35 = bf16[2,216,1536]{2,1,0:T(8,128)(2,1)S(1)} collective-permute-done((bf16[2,216,1536]{2,1,0:T(8,128)(2,1)S(1)}, bf16[2,216,1536]{2,1,0:T(8,128)(2,1)S(1)}, u32[]{:S(2)}, u32[]{:S(2)}) %collective-permute-start.35) | collective-permute-done | bytes 1327136 | tf_op jit(solution)/shard_map/ppermute | solution.py:108
  415.4 10.0 collective-permute-done.20
  426.6 11.4 collective-permute-done.50
  441.9 23.8 %collective-permute-done.33 = bf16[2,2,192,864]{3,2,1,0:T(8,128)(2,1)S(1)} collective-permute-done((bf16[2,2,192,864]{3,2,1,0:T(8,128)(2,1)S(1)}, bf16[2,2,192,864]{3,2,1,0:T(8,128)(2,1)S(1)}, u32[]{:S(2)}, u32[]{:S(2)}) %collective-permute-start.33) | collective-permute-done | bytes 1327136 | tf_op jit(solution)/shard_map/ppermute | solution.py:108
  467.9 19.8 %collective-permute-done.47 = bf16[2,2,192,640]{3,2,1,0:T(8,128)(2,1)S(1)} collective-permute-done((bf16[2,2,192,640]{3,2,1,0:T(8,128)(2,1)S(1)}, bf16[2,2,192,640]{3,2,1,0:T(8,128)(2,1)S(1)}, u32[]{:S(2)}, u32[]{:S(2)}) %collective-permute-start.47) | collective-permute-done | bytes 983072 | tf_op jit(solution)/shard_map/ppermute | solution.py:108
  496.6 24.1 %collective-permute-done.62 = bf16[2,2,192,864]{3,2,1,0:T(8,128)(2,1)S(1)} collective-permute-done((bf16[2,2,192,864]{3,2,1,0:T(8,128)(2,1)S(1)}, bf16[2,2,192,864]{3,2,1,0:T(8,128)(2,1)S(1)}, u32[]{:S(2)}, u32[]{:S(2)}) %collective-permute-start.62) | collective-permute-done | bytes 1327136 | tf_op jit(solution)/shard_map/ppermute | solution.py:108
  523.5 26.8 %collective-permute-done.65 = bf16[2,2,192,864]{3,2,1,0:T(8,128)(2,1)} collective-permute-done((bf16[2,2,192,864]{3,2,1,0:T(8,128)(2,1)}, bf16[2,2,192,864]{3,2,1,0:T(8,128)(2,1)}, u32[]{:S(2)}, u32[]{:S(2)}) %collective-permute-start.65) | collective-permute-done | bytes 1327136 | tf_op jit(solution)/shard_map/ppermute | solution.py:108
  556.5 18.7 %collective-permute-done.67 = bf16[2,216,1536]{2,1,0:T(8,128)(2,1)} collective-permute-done((bf16[2,216,1536]{2,1,0:T(8,128)(2,1)}, bf16[2,216,1536]{2,1,0:T(8,128)(2,1)}, u32[]{:S(2)}, u32[]{:S(2)}) %collective-permute-start.67) | collective-permute-done | bytes 1327136 | tf_op jit(solution)/shard_map/ppermute | solution.py:108
  591.9 6.2 multiply_convert_fusion.3
  613.2 10.5 collective-permute-done.38
  626.9 21.3 %collective-permute-done.41 = f32[160,1536]{1,0:T(8,128)S(1)} collective-permute-done((f32[160,1536]{1,0:T(8,128)S(1)}, f32[160,1536]{1,0:T(8,128)S(1)}, u32[]{:S(2)}, u32[]{:S(2)}) %collective-permute-start.41) | collective-permute-done | bytes 983072 | tf_op jit(solution)/shard_map/ppermute | solution.py:108
  653.1 10.5 collective-permute-done.42
  695.9 20.3 %collective-permute-done.53 = f32[160,1536]{1,0:T(8,128)S(1)} collective-permute-done((f32[160,1536]{1,0:T(8,128)S(1)}, f32[160,1536]{1,0:T(8,128)S(1)}, u32[]{:S(2)}, u32[]{:S(2)}) %collective-permute-start.53) | collective-permute-done | bytes 983072 | tf_op jit(solution)/shard_map/ppermute | solution.py:108
  720.1 9.5 collective-permute-done.55
  737.8 6.9 collective-permute-done.57
  752.9 13.2 fusion.13
  766.1 7.1 convolution_convert_fusion.2
  782.5 6.5 fusion.134
  797.5 6.5 fusion.135
  825.4 13.0 collective-permute-done.115
  839.9 27.3 %collective-permute-done.110 = bf16[2,2,192,864]{3,2,1,0:T(8,128)(2,1)S(1)} collective-permute-done((bf16[2,2,192,864]{3,2,1,0:T(8,128)(2,1)S(1)}, bf16[2,2,192,864]{3,2,1,0:T(8,128)(2,1)S(1)}, u32[]{:S(2)}, u32[]{:S(2)}) %collective-permute-start.110) | collective-permute-done | bytes 1327136 | tf_op jit(solution)/shard_map/ppermute | solution.py:108
  883.1 31.4 %collective-permute-done.85 = bf16[160,1536]{1,0:T(8,128)(2,1)S(1)} collective-permute-done((bf16[160,1536]{1,0:T(8,128)(2,1)S(1)}, bf16[160,1536]{1,0:T(8,128)(2,1)S(1)}, u32[]{:S(2)}, u32[]{:S(2)}) %collective-permute-start.85) | collective-permute-done | bytes 491552 | tf_op jit(solution)/shard_map/ppermute | solution.py:108
  918.9 27.0 %collective-permute-done.73 = bf16[160,1536]{1,0:T(8,128)(2,1)S(1)} collective-permute-done((bf16[160,1536]{1,0:T(8,128)(2,1)S(1)}, bf16[160,1536]{1,0:T(8,128)(2,1)S(1)}, u32[]{:S(2)}, u32[]{:S(2)}) %collective-permute-start.73) | collective-permute-done | bytes 491552 | tf_op jit(solution)/shard_map/ppermute | solution.py:108
  949.1 11.7 collective-permute-done.86
  989.7 10.7 fusion.2
  1055.2 18.3 %collective-permute-done.93 = bf16[160,1536]{1,0:T(8,128)(2,1)S(1)} collective-permute-done((bf16[160,1536]{1,0:T(8,128)(2,1)S(1)}, bf16[160,1536]{1,0:T(8,128)(2,1)S(1)}, u32[]{:S(2)}, u32[]{:S(2)}) %collective-permute-start.93) | collective-permute-done | bytes 491552 | tf_op jit(solution)/shard_map/ppermute | solution.py:108
  1101.7 7.6 fusion.16
  1121.0 6.5 fusion.136
  1161.0 15.4 %collective-permute-done.118 = bf16[2,2,192,864]{3,2,1,0:T(8,128)(2,1)S(1)} collective-permute-done((bf16[2,2,192,864]{3,2,1,0:T(8,128)(2,1)S(1)}, bf16[2,2,192,864]{3,2,1,0:T(8,128)(2,1)S(1)}, u32[]{:S(2)}, u32[]{:S(2)}) %collective-permute-start.118) | collective-permute-done | bytes 1327136 | tf_op jit(solution)/shard_map/ppermute | solution.py:108
  1186.0 34.4 %collective-permute-done.129 = bf16[2,192,864]{2,1,0:T(8,128)(2,1)} collective-permute-done((bf16[2,192,864]{2,1,0:T(8,128)(2,1)}, bf16[2,192,864]{2,1,0:T(8,128)(2,1)}, u32[]{:S(2)}, u32[]{:S(2)}) %collective-permute-start.129) | collective-permute-done | bytes 663584 | tf_op jit(solution)/shard_map/ppermute | solution.py:108
  1263.1 11.4 collective-permute-done.130
  1310.3 11.4 collective-permute-done.114
  1333.2 33.5 %collective-permute-done.132 = bf16[2,192,1152]{2,1,0:T(8,128)(2,1)S(1)} collective-permute-done((bf16[2,192,1152]{2,1,0:T(8,128)(2,1)S(1)}, bf16[2,192,1152]{2,1,0:T(8,128)(2,1)S(1)}, u32[]{:S(2)}, u32[]{:S(2)}) %collective-permute-start.132) | collective-permute-done | bytes 884768 | tf_op jit(solution)/shard_map/ppermute | solution.py:108
  1367.2 11.2 collective-permute-done.137
  1393.4 39.7 %moments_pass.1 = (f32[1,1,2482320]{2,1,0:T(1,128)}, f32[1,1,2482320]{2,1,0:T(1,128)}, f32[1,1,2482320]{2,1,0:T(1,128)}, f32[28,8,128]{2,1,0:T(8,128)}) custom-call(s32[2,204]{1,0:T(2,128)} %constant.673.clone.table, f32[1,1,2482320]{2,1,0:T(1,128)} %w_ref.3, f32[1,1,2482320]{2,1,0:T(1,128)} %m_ref.1, f32[1,1,2482320]{2,1,0:T(1,128)} %v_ref.1, ...), custom_call_target="tpu_custom_call" | custom-call | flops 49646400 | bytes 69504960 | tf_op jit(solution)/shard_map/moments_pass/pallas_call | solution.py:484
  1455.0 32.1 %weights_pass.1 = (f32[1,1,2482320]{2,1,0:T(1,128)}, bf16[1,1,2482320]{2,1,0:T(2,128)(2,1)}) custom-call(s32[2,204]{1,0:T(2,128)} %constant.673.clone.table, f32[1,1,2482320]{2,1,0:T(1,128)} %w_ref.3, f32[1,1,2482320]{2,1,0:T(1,128)} %get-tuple-element.58.m_ref, f32[1,1,2482320]{2,1,0:T(1,128)} %get-tuple-element.59.v_ref, f32[14]{0:T(128)} %pad_maximum_fusion.39.ratio_ref), custom_call_target="tpu_custom_call" | custom-call | flops 19858560 | bytes 44681760 | tf_op jit(solution)/shard_map/weights_pass/pallas_call | solution.py:530
  (1144 shorter events, 610.2 us)
Async XLA Ops:
  2.1 80.4 %collective-permute-start.6 = (f32[340]{0:T(512)S(1)}, f32[340]{0:T(512)S(1)}, u32[]{:S(2)}, u32[]{:S(2)}) collective-permute-start(f32[340]{0:T(512)S(1)} %pad_maximum_fusion.36), channel_id=1, source_target_pairs={{0,28},{4,24},{8,20},{12,16},{16,12},{20,8},{24,4},{28,0},{1,29},{... | collective-permute-start | bytes 4088 | tf_op jit(solution)/shard_map/ppermute | solution.py:108
  8.1 78.3 %collective-permute-start.5 = (f32[340]{0:T(512)S(1)}, f32[340]{0:T(512)}, u32[]{:S(2)}, u32[]{:S(2)}) collective-permute-start(f32[340]{0:T(512)S(1)} %pad_maximum_fusion.36), channel_id=1, source_target_pairs={{0,24},{4,28},{8,16},{12,20},{16,8},{20,12},{24,0},{28,4},{1,25},{... | collective-permute-start | bytes 4088 | tf_op jit(solution)/shard_map/ppermute | solution.py:108
  8.3 81.0 %collective-permute-start.4 = (f32[340]{0:T(512)S(1)}, f32[340]{0:T(512)}, u32[]{:S(2)}, u32[]{:S(2)}) collective-permute-start(f32[340]{0:T(512)S(1)} %pad_maximum_fusion.36), channel_id=1, source_target_pairs={{0,20},{4,16},{8,28},{12,24},{16,4},{20,0},{24,12},{28,8},{1,21},{... | collective-permute-start | bytes 4088 | tf_op jit(solution)/shard_map/ppermute | solution.py:108
  59.2 48.8 %collective-permute-start.14 = (bf16[2,192,1152]{2,1,0:T(8,128)(2,1)S(1)}, bf16[2,192,1152]{2,1,0:T(8,128)(2,1)}, u32[]{:S(2)}, u32[]{:S(2)}) collective-permute-start(bf16[2,192,1152]{2,1,0:T(8,128)(2,1)S(1)} %broadcast_select_fusion.11), channel_id=1, source_target_pairs={{0,16},{4,20},{8,24},{12,28},{16,0},{20,4},{24,8},{28,12},{1,17},{... | collective-permute-start | bytes 2654216 | tf_op jit(solution)/shard_map/ppermute | solution.py:108
  122.1 58.1 %collective-permute-start.30 = (bf16[2,192,864]{2,1,0:T(8,128)(2,1)S(1)}, bf16[2,192,864]{2,1,0:T(8,128)(2,1)}, u32[]{:S(2)}, u32[]{:S(2)}) collective-permute-start(bf16[2,192,864]{2,1,0:T(8,128)(2,1)S(1)} %get-tuple-element.70), channel_id=1, source_target_pairs={{0,16},{4,20},{8,24},{12,28},{16,0},{20,4},{24,8},{28,12},{1,17},{... | collective-permute-start | bytes 1990664 | tf_op jit(solution)/shard_map/ppermute | solution.py:108
  150.6 58.6 %collective-permute-start.32 = (bf16[2,192,864]{2,1,0:T(8,128)(2,1)S(1)}, bf16[2,192,864]{2,1,0:T(8,128)(2,1)}, u32[]{:S(2)}, u32[]{:S(2)}) collective-permute-start(bf16[2,192,864]{2,1,0:T(8,128)(2,1)S(1)} %get-tuple-element.72), channel_id=1, source_target_pairs={{0,16},{4,20},{8,24},{12,28},{16,0},{20,4},{24,8},{28,12},{1,17},{... | collective-permute-start | bytes 1990664 | tf_op jit(solution)/shard_map/ppermute | solution.py:108
  180.2 49.6 %collective-permute-start.34 = (bf16[216,1536]{1,0:T(8,128)(2,1)S(1)}, bf16[216,1536]{1,0:T(8,128)(2,1)}, u32[]{:S(2)}, u32[]{:S(2)}) collective-permute-start(bf16[216,1536]{1,0:T(8,128)(2,1)S(1)} %broadcast_in_dim.846), channel_id=1, source_target_pairs={{0,16},{4,20},{8,24},{12,28},{16,0},{20,4},{24,8},{28,12},{1,17},{... | collective-permute-start | bytes 1990664 | tf_op jit(solution)/shard_map/ppermute | solution.py:108
  270.9 77.6 %collective-permute-start.15 = (bf16[2,2,192,1152]{3,2,1,0:T(8,128)(2,1)S(1)}, bf16[2,2,192,1152]{3,2,1,0:T(8,128)(2,1)}, u32[]{:S(2)}, u32[]{:S(2)}) collective-permute-start(bf16[2,2,192,1152]{3,2,1,0:T(8,128)(2,1)S(1)} %broadcast_select_fusion.1), channel_id=1, source_target_pairs={{0,4},{4,0},{8,12},{12,8},{16,20},{20,16},{24,28},{28,24},{1,5},{5... | collective-permute-start | bytes 5308424 | tf_op jit(solution)/shard_map/ppermute | solution.py:108
  282.8 61.9 %collective-permute-start.64 = (bf16[2,192,864]{2,1,0:T(8,128)(2,1)}, bf16[2,192,864]{2,1,0:T(8,128)(2,1)}, u32[]{:S(2)}, u32[]{:S(2)}) collective-permute-start(bf16[2,192,864]{2,1,0:T(8,128)(2,1)} %get-tuple-element.86), channel_id=1, source_target_pairs={{0,16},{4,20},{8,24},{12,28},{16,0},{20,4},{24,8},{28,12},{1,17},{... | collective-permute-start | bytes 1990664 | tf_op jit(solution)/shard_map/ppermute | solution.py:108
  283.3 61.4 %collective-permute-start.61 = (bf16[2,192,864]{2,1,0:T(8,128)(2,1)}, bf16[2,192,864]{2,1,0:T(8,128)(2,1)}, u32[]{:S(2)}, u32[]{:S(2)}) collective-permute-start(bf16[2,192,864]{2,1,0:T(8,128)(2,1)} %get-tuple-element.83), channel_id=1, source_target_pairs={{0,16},{4,20},{8,24},{12,28},{16,0},{20,4},{24,8},{28,12},{1,17},{... | collective-permute-start | bytes 1990664 | tf_op jit(solution)/shard_map/ppermute | solution.py:108
  344.7 30.9 %collective-permute-start.66 = (bf16[216,1536]{1,0:T(8,128)(2,1)S(1)}, bf16[216,1536]{1,0:T(8,128)(2,1)S(1)}, u32[]{:S(2)}, u32[]{:S(2)}) collective-permute-start(bf16[216,1536]{1,0:T(8,128)(2,1)S(1)} %copy-done.82), channel_id=1, source_target_pairs={{0,16},{4,20},{8,24},{12,28},{16,0},{20,4},{24,8},{28,12},{1,17},{... | collective-permute-start | bytes 1990664 | tf_op jit(solution)/shard_map/ppermute | solution.py:108
  348.5 32.2 %collective-permute-start.31 = (bf16[2,2,192,864]{3,2,1,0:T(8,128)(2,1)S(1)}, bf16[2,2,192,864]{3,2,1,0:T(8,128)(2,1)S(1)}, u32[]{:S(2)}, u32[]{:S(2)}) collective-permute-start(bf16[2,2,192,864]{3,2,1,0:T(8,128)(2,1)S(1)} %get-tuple-element.71), channel_id=1, source_target_pairs={{0,4},{4,0},{8,12},{12,8},{16,20},{20,16},{24,28},{28,24},{1,5},{5... | collective-permute-start | bytes 3981320 | tf_op jit(solution)/shard_map/ppermute | solution.py:108
  380.7 32.0 %collective-permute-start.35 = (bf16[2,216,1536]{2,1,0:T(8,128)(2,1)S(1)}, bf16[2,216,1536]{2,1,0:T(8,128)(2,1)S(1)}, u32[]{:S(2)}, u32[]{:S(2)}) collective-permute-start(bf16[2,216,1536]{2,1,0:T(8,128)(2,1)S(1)} %get-tuple-element.75), channel_id=1, source_target_pairs={{0,4},{4,0},{8,12},{12,8},{16,20},{20,16},{24,28},{28,24},{1,5},{5... | collective-permute-start | bytes 3981320 | tf_op jit(solution)/shard_map/ppermute | solution.py:108
  387.0 38.4 %collective-permute-start.20 = (bf16[2,2,48,1536]{3,2,1,0:T(8,128)(2,1)S(1)}, bf16[2,2,48,1536]{3,2,1,0:T(8,128)(2,1)S(1)}, u32[]{:S(2)}, u32[]{:S(2)}) collective-permute-start(bf16[2,2,48,1536]{3,2,1,0:T(8,128)(2,1)S(1)} %get-tuple-element.297), channel_id=1, source_target_pairs={{0,4},{4,0},{8,12},{12,8},{16,20},{20,16},{24,28},{28,24},{1,5},{5... | collective-permute-start | bytes 1769480 | tf_op jit(solution)/shard_map/ppermute | solution.py:108
  425.4 40.3 %collective-permute-start.33 = (bf16[2,2,192,864]{3,2,1,0:T(8,128)(2,1)S(1)}, bf16[2,2,192,864]{3,2,1,0:T(8,128)(2,1)S(1)}, u32[]{:S(2)}, u32[]{:S(2)}) collective-permute-start(bf16[2,2,192,864]{3,2,1,0:T(8,128)(2,1)S(1)} %get-tuple-element.73), channel_id=1, source_target_pairs={{0,4},{4,0},{8,12},{12,8},{16,20},{20,16},{24,28},{28,24},{1,5},{5... | collective-permute-start | bytes 3981320 | tf_op jit(solution)/shard_map/ppermute | solution.py:108
  487.7 33.1 %collective-permute-start.62 = (bf16[2,2,192,864]{3,2,1,0:T(8,128)(2,1)S(1)}, bf16[2,2,192,864]{3,2,1,0:T(8,128)(2,1)S(1)}, u32[]{:S(2)}, u32[]{:S(2)}) collective-permute-start(bf16[2,2,192,864]{3,2,1,0:T(8,128)(2,1)S(1)} %get-tuple-element.84), channel_id=1, source_target_pairs={{0,4},{4,0},{8,12},{12,8},{16,20},{20,16},{24,28},{28,24},{1,5},{5... | collective-permute-start | bytes 3981320 | tf_op jit(solution)/shard_map/ppermute | solution.py:108
  495.8 54.5 %collective-permute-start.65 = (bf16[2,2,192,864]{3,2,1,0:T(8,128)(2,1)}, bf16[2,2,192,864]{3,2,1,0:T(8,128)(2,1)}, u32[]{:S(2)}, u32[]{:S(2)}) collective-permute-start(bf16[2,2,192,864]{3,2,1,0:T(8,128)(2,1)} %get-tuple-element.87), channel_id=1, source_target_pairs={{0,4},{4,0},{8,12},{12,8},{16,20},{20,16},{24,28},{28,24},{1,5},{5... | collective-permute-start | bytes 3981320 | tf_op jit(solution)/shard_map/ppermute | solution.py:108
  520.7 54.5 %collective-permute-start.67 = (bf16[2,216,1536]{2,1,0:T(8,128)(2,1)}, bf16[2,216,1536]{2,1,0:T(8,128)(2,1)}, u32[]{:S(2)}, u32[]{:S(2)}) collective-permute-start(bf16[2,216,1536]{2,1,0:T(8,128)(2,1)} %get-tuple-element.89), channel_id=1, source_target_pairs={{0,4},{4,0},{8,12},{12,8},{16,20},{20,16},{24,28},{28,24},{1,5},{5... | collective-permute-start | bytes 3981320 | tf_op jit(solution)/shard_map/ppermute | solution.py:108
  523.1 63.1 %collective-permute-start.26 = (bf16[480,1536]{1,0:T(8,128)(2,1)}, bf16[480,1536]{1,0:T(8,128)(2,1)}, u32[]{:S(2)}, u32[]{:S(2)}) collective-permute-start(bf16[480,1536]{1,0:T(8,128)(2,1)} %pad_maximum_fusion.4), channel_id=1, source_target_pairs={{0,1},{1,0},{2,3},{3,2},{4,5},{5,4},{6,7},{7,6},{8,9},{9,8},{10,11... | collective-permute-start | bytes 4423688 | tf_op jit(solution)/shard_map/ppermute | solution.py:108
  650.0 36.5 %collective-permute-start.75 = (bf16[160,1536]{1,0:T(8,128)(2,1)S(1)}, bf16[160,1536]{1,0:T(8,128)(2,1)S(1)}, u32[]{:S(2)}, u32[]{:S(2)}) collective-permute-start(bf16[160,1536]{1,0:T(8,128)(2,1)S(1)} %copy-done.24), channel_id=1, source_target_pairs={{0,8},{4,12},{8,0},{12,4},{16,24},{20,28},{24,16},{28,20},{1,9},{5... | collective-permute-start | bytes 1474568 | tf_op jit(solution)/shard_map/ppermute | solution.py:108
  651.3 35.2 %collective-permute-start.74 = (bf16[160,1536]{1,0:T(8,128)(2,1)S(1)}, bf16[160,1536]{1,0:T(8,128)(2,1)S(1)}, u32[]{:S(2)}, u32[]{:S(2)}) collective-permute-start(bf16[160,1536]{1,0:T(8,128)(2,1)S(1)} %copy-done.24), channel_id=1, source_target_pairs={{0,2},{1,3},{2,0},{3,1},{4,6},{5,7},{6,4},{7,5},{8,10},{9,11},{10,... | collective-permute-start | bytes 1474568 | tf_op jit(solution)/shard_map/ppermute | solution.py:108
  806.2 32.2 %collective-permute-start.115 = (bf16[2,216,1536]{2,1,0:T(8,128)(2,1)S(1)}, bf16[2,216,1536]{2,1,0:T(8,128)(2,1)}, u32[]{:S(2)}, u32[]{:S(2)}) collective-permute-start(bf16[2,216,1536]{2,1,0:T(8,128)(2,1)S(1)} %dynamic-slice_bitcast_fusion.5), channel_id=1, source_target_pairs={{0,4},{4,0},{8,12},{12,8},{16,20},{20,16},{24,28},{28,24},{1,5},{5... | collective-permute-start | bytes 3981320 | tf_op jit(solution)/shard_map/ppermute | solution.py:108
  818.2 49.0 %collective-permute-start.110 = (bf16[2,2,192,864]{3,2,1,0:T(8,128)(2,1)S(1)}, bf16[2,2,192,864]{3,2,1,0:T(8,128)(2,1)S(1)}, u32[]{:S(2)}, u32[]{:S(2)}) collective-permute-start(bf16[2,2,192,864]{3,2,1,0:T(8,128)(2,1)S(1)} %dynamic-slice_bitcast_fusion.3), channel_id=1, source_target_pairs={{0,4},{4,0},{8,12},{12,8},{16,20},{20,16},{24,28},{28,24},{1,5},{5... | collective-permute-start | bytes 3981320 | tf_op jit(solution)/shard_map/ppermute | solution.py:108
  819.1 51.5 %collective-permute-start.80 = (bf16[480,1536]{1,0:T(8,128)(2,1)}, bf16[480,1536]{1,0:T(8,128)(2,1)S(1)}, u32[]{:S(2)}, u32[]{:S(2)}) collective-permute-start(bf16[480,1536]{1,0:T(8,128)(2,1)} %slice.615), channel_id=1, source_target_pairs={{0,1},{1,0},{2,3},{3,2},{4,5},{5,4},{6,7},{7,6},{8,9},{9,8},{10,11... | collective-permute-start | bytes 4423688 | tf_op jit(solution)/shard_map/ppermute | solution.py:108
  820.9 53.7 %collective-permute-start.68 = (bf16[480,1536]{1,0:T(8,128)(2,1)S(1)}, bf16[480,1536]{1,0:T(8,128)(2,1)S(1)}, u32[]{:S(2)}, u32[]{:S(2)}) collective-permute-start(bf16[480,1536]{1,0:T(8,128)(2,1)S(1)} %copy-done.101), channel_id=1, source_target_pairs={{0,1},{1,0},{2,3},{3,2},{4,5},{5,4},{6,7},{7,6},{8,9},{9,8},{10,11... | collective-permute-start | bytes 4423688 | tf_op jit(solution)/shard_map/ppermute | solution.py:108
  823.3 54.7 %collective-permute-start.82 = (bf16[80,1536]{1,0:T(8,128)(2,1)S(1)}, bf16[80,1536]{1,0:T(8,128)(2,1)S(1)}, u32[]{:S(2)}, u32[]{:S(2)}) collective-permute-start(bf16[80,1536]{1,0:T(8,128)(2,1)S(1)} %get-tuple-element.257), channel_id=1, source_target_pairs={{0,8},{4,12},{8,0},{12,4},{16,24},{20,28},{24,16},{28,20},{1,9},{5... | collective-permute-start | bytes 737288 | tf_op jit(solution)/shard_map/ppermute | solution.py:108
  838.4 40.9 %collective-permute-start.84 = (bf16[80,1536]{1,0:T(8,128)(2,1)S(1)}, bf16[80,1536]{1,0:T(8,128)(2,1)S(1)}, u32[]{:S(2)}, u32[]{:S(2)}) collective-permute-start(bf16[80,1536]{1,0:T(8,128)(2,1)S(1)} %get-tuple-element.258), channel_id=1, source_target_pairs={{0,2},{1,3},{2,0},{3,1},{4,6},{5,7},{6,4},{7,5},{8,10},{9,11},{10,... | collective-permute-start | bytes 737288 | tf_op jit(solution)/shard_map/ppermute | solution.py:108
  874.6 74.5 %collective-permute-start.124 = (bf16[216,1536]{1,0:T(8,128)(2,1)S(1)}, bf16[216,1536]{1,0:T(8,128)(2,1)S(1)}, u32[]{:S(2)}, u32[]{:S(2)}) collective-permute-start(bf16[216,1536]{1,0:T(8,128)(2,1)S(1)} %dynamic-slice_bitcast_fusion.14), channel_id=1, source_target_pairs={{0,16},{4,20},{8,24},{12,28},{16,0},{20,4},{24,8},{28,12},{1,17},{... | collective-permute-start | bytes 1990664 | tf_op jit(solution)/shard_map/ppermute | solution.py:108
  878.0 97.0 %collective-permute-start.116 = (bf16[2,2,192,864]{3,2,1,0:T(8,128)(2,1)}, bf16[2,2,192,864]{3,2,1,0:T(8,128)(2,1)}, u32[]{:S(2)}, u32[]{:S(2)}) collective-permute-start(bf16[2,2,192,864]{3,2,1,0:T(8,128)(2,1)} %dynamic-slice_bitcast_fusion.1), channel_id=1, source_target_pairs={{0,4},{4,0},{8,12},{12,8},{16,20},{20,16},{24,28},{28,24},{1,5},{5... | collective-permute-start | bytes 3981320 | tf_op jit(solution)/shard_map/ppermute | solution.py:108
  879.3 68.7 %collective-permute-start.120 = (bf16[2,192,864]{2,1,0:T(8,128)(2,1)S(1)}, bf16[2,192,864]{2,1,0:T(8,128)(2,1)S(1)}, u32[]{:S(2)}, u32[]{:S(2)}) collective-permute-start(bf16[2,192,864]{2,1,0:T(8,128)(2,1)S(1)} %dynamic-slice_bitcast_fusion.9), channel_id=1, source_target_pairs={{0,16},{4,20},{8,24},{12,28},{16,0},{20,4},{24,8},{28,12},{1,17},{... | collective-permute-start | bytes 1990664 | tf_op jit(solution)/shard_map/ppermute | solution.py:108
  881.5 33.0 %collective-permute-start.85 = (bf16[160,1536]{1,0:T(8,128)(2,1)S(1)}, bf16[160,1536]{1,0:T(8,128)(2,1)S(1)}, u32[]{:S(2)}, u32[]{:S(2)}) collective-permute-start(bf16[160,1536]{1,0:T(8,128)(2,1)S(1)} %pad_maximum_fusion.20), channel_id=1, source_target_pairs={{0,8},{4,12},{8,0},{12,4},{16,24},{20,28},{24,16},{28,20},{1,9},{5... | collective-permute-start | bytes 1474568 | tf_op jit(solution)/shard_map/ppermute | solution.py:108
  882.3 34.7 %collective-permute-start.83 = (bf16[160,1536]{1,0:T(8,128)(2,1)S(1)}, bf16[160,1536]{1,0:T(8,128)(2,1)S(1)}, u32[]{:S(2)}, u32[]{:S(2)}) collective-permute-start(bf16[160,1536]{1,0:T(8,128)(2,1)S(1)} %pad_maximum_fusion.19), channel_id=1, source_target_pairs={{0,2},{1,3},{2,0},{3,1},{4,6},{5,7},{6,4},{7,5},{8,10},{9,11},{10,... | collective-permute-start | bytes 1474568 | tf_op jit(solution)/shard_map/ppermute | solution.py:108
  914.5 31.4 %collective-permute-start.73 = (bf16[160,1536]{1,0:T(8,128)(2,1)S(1)}, bf16[160,1536]{1,0:T(8,128)(2,1)S(1)}, u32[]{:S(2)}, u32[]{:S(2)}) collective-permute-start(bf16[160,1536]{1,0:T(8,128)(2,1)S(1)} %pad_maximum_fusion.17), channel_id=1, source_target_pairs={{0,8},{4,12},{8,0},{12,4},{16,24},{20,28},{24,16},{28,20},{1,9},{5... | collective-permute-start | bytes 1474568 | tf_op jit(solution)/shard_map/ppermute | solution.py:108
  947.9 31.4 %collective-permute-start.87 = (bf16[160,1536]{1,0:T(8,128)(2,1)}, bf16[160,1536]{1,0:T(8,128)(2,1)}, u32[]{:S(2)}, u32[]{:S(2)}) collective-permute-start(bf16[160,1536]{1,0:T(8,128)(2,1)} %get-tuple-element.237), channel_id=1, source_target_pairs={{0,1},{1,0},{2,3},{3,2},{4,5},{5,4},{6,7},{7,6},{8,9},{9,8},{10,11... | collective-permute-start | bytes 1474568 | tf_op jit(solution)/shard_map/ppermute | solution.py:108
  979.3 39.1 %collective-permute-start.121 = (bf16[2,192,864]{2,1,0:T(8,128)(2,1)}, bf16[2,192,864]{2,1,0:T(8,128)(2,1)}, u32[]{:S(2)}, u32[]{:S(2)}) collective-permute-start(bf16[2,192,864]{2,1,0:T(8,128)(2,1)} %dynamic-slice_bitcast_fusion.10), channel_id=1, source_target_pairs={{0,16},{4,20},{8,24},{12,28},{16,0},{20,4},{24,8},{28,12},{1,17},{... | collective-permute-start | bytes 1990664 | tf_op jit(solution)/shard_map/ppermute | solution.py:108
  1079.8 98.7 %collective-permute-start.128 = (bf16[192,640]{1,0:T(8,128)(2,1)S(1)}, bf16[192,640]{1,0:T(8,128)(2,1)}, u32[]{:S(2)}, u32[]{:S(2)}) collective-permute-start(bf16[192,640]{1,0:T(8,128)(2,1)S(1)} %dynamic-slice_bitcast_fusion.25), channel_id=1, source_target_pairs={{0,8},{4,12},{8,0},{12,4},{16,24},{20,28},{24,16},{28,20},{1,9},{5... | collective-permute-start | bytes 737288 | tf_op jit(solution)/shard_map/ppermute | solution.py:108
  1110.4 38.2 %collective-permute-start.112 = (bf16[2,216,1536]{2,1,0:T(8,128)(2,1)}, bf16[2,216,1536]{2,1,0:T(8,128)(2,1)}, u32[]{:S(2)}, u32[]{:S(2)}) collective-permute-start(bf16[2,216,1536]{2,1,0:T(8,128)(2,1)} %dynamic-slice_bitcast_fusion.6), channel_id=1, source_target_pairs={{0,4},{4,0},{8,12},{12,8},{16,20},{20,16},{24,28},{28,24},{1,5},{5... | collective-permute-start | bytes 3981320 | tf_op jit(solution)/shard_map/ppermute | solution.py:108
  1143.8 32.6 %collective-permute-start.118 = (bf16[2,2,192,864]{3,2,1,0:T(8,128)(2,1)S(1)}, bf16[2,2,192,864]{3,2,1,0:T(8,128)(2,1)S(1)}, u32[]{:S(2)}, u32[]{:S(2)}) collective-permute-start(bf16[2,2,192,864]{3,2,1,0:T(8,128)(2,1)S(1)} %dynamic-slice_bitcast_fusion.2), channel_id=1, source_target_pairs={{0,4},{4,0},{8,12},{12,8},{16,20},{20,16},{24,28},{28,24},{1,5},{5... | collective-permute-start | bytes 3981320 | tf_op jit(solution)/shard_map/ppermute | solution.py:108
  1160.0 62.7 %collective-permute-start.133 = (bf16[216,1536]{1,0:T(8,128)(2,1)}, bf16[216,1536]{1,0:T(8,128)(2,1)}, u32[]{:S(2)}, u32[]{:S(2)}) collective-permute-start(bf16[216,1536]{1,0:T(8,128)(2,1)} %dynamic-slice_bitcast_fusion.13), channel_id=1, source_target_pairs={{0,16},{4,20},{8,24},{12,28},{16,0},{20,4},{24,8},{28,12},{1,17},{... | collective-permute-start | bytes 1990664 | tf_op jit(solution)/shard_map/ppermute | solution.py:108
  1176.4 62.6 %collective-permute-start.113 = (bf16[2,2,192,864]{3,2,1,0:T(8,128)(2,1)}, bf16[2,2,192,864]{3,2,1,0:T(8,128)(2,1)}, u32[]{:S(2)}, u32[]{:S(2)}) collective-permute-start(bf16[2,2,192,864]{3,2,1,0:T(8,128)(2,1)} %dynamic-slice_bitcast_fusion.4), channel_id=1, source_target_pairs={{0,4},{4,0},{8,12},{12,8},{16,20},{20,16},{24,28},{28,24},{1,5},{5... | collective-permute-start | bytes 3981320 | tf_op jit(solution)/shard_map/ppermute | solution.py:108
  1178.5 41.9 %collective-permute-start.129 = (bf16[2,192,864]{2,1,0:T(8,128)(2,1)}, bf16[2,192,864]{2,1,0:T(8,128)(2,1)}, u32[]{:S(2)}, u32[]{:S(2)}) collective-permute-start(bf16[2,192,864]{2,1,0:T(8,128)(2,1)} %dynamic-slice_bitcast_fusion.11), channel_id=1, source_target_pairs={{0,16},{4,20},{8,24},{12,28},{16,0},{20,4},{24,8},{28,12},{1,17},{... | collective-permute-start | bytes 1990664 | tf_op jit(solution)/shard_map/ppermute | solution.py:108
  1182.4 40.3 %collective-permute-start.104 = (bf16[160,1536]{1,0:T(8,128)(2,1)}, bf16[160,1536]{1,0:T(8,128)(2,1)}, u32[]{:S(2)}, u32[]{:S(2)}) collective-permute-start(bf16[160,1536]{1,0:T(8,128)(2,1)} %get-tuple-element.164), channel_id=1, source_target_pairs={{0,2},{1,3},{2,0},{3,1},{4,6},{5,7},{6,4},{7,5},{8,10},{9,11},{10,... | collective-permute-start | bytes 1474568 | tf_op jit(solution)/shard_map/ppermute | solution.py:108
  1186.0 57.1 %collective-permute-start.105 = (bf16[160,1536]{1,0:T(8,128)(2,1)}, bf16[160,1536]{1,0:T(8,128)(2,1)}, u32[]{:S(2)}, u32[]{:S(2)}) collective-permute-start(bf16[160,1536]{1,0:T(8,128)(2,1)} %get-tuple-element.164), channel_id=1, source_target_pairs={{0,1},{1,0},{2,3},{3,2},{4,5},{5,4},{6,7},{7,6},{8,9},{9,8},{10,11... | collective-permute-start | bytes 1474568 | tf_op jit(solution)/shard_map/ppermute | solution.py:108
  1240.9 33.5 %collective-permute-start.130 = (bf16[2,192,864]{2,1,0:T(8,128)(2,1)S(1)}, bf16[2,192,864]{2,1,0:T(8,128)(2,1)S(1)}, u32[]{:S(2)}, u32[]{:S(2)}) collective-permute-start(bf16[2,192,864]{2,1,0:T(8,128)(2,1)S(1)} %dynamic-slice_bitcast_fusion.12), channel_id=1, source_target_pairs={{0,16},{4,20},{8,24},{12,28},{16,0},{20,4},{24,8},{28,12},{1,17},{... | collective-permute-start | bytes 1990664 | tf_op jit(solution)/shard_map/ppermute | solution.py:108
  1256.2 41.1 %collective-permute-start.107 = (bf16[160,1536]{1,0:T(8,128)(2,1)}, bf16[160,1536]{1,0:T(8,128)(2,1)}, u32[]{:S(2)}, u32[]{:S(2)}) collective-permute-start(bf16[160,1536]{1,0:T(8,128)(2,1)} %get-tuple-element.218), channel_id=1, source_target_pairs={{0,1},{1,0},{2,3},{3,2},{4,5},{5,4},{6,7},{7,6},{8,9},{9,8},{10,11... | collective-permute-start | bytes 1474568 | tf_op jit(solution)/shard_map/ppermute | solution.py:108
  1281.9 39.8 %collective-permute-start.114 = (bf16[2,2,192,1152]{3,2,1,0:T(8,128)(2,1)}, bf16[2,2,192,1152]{3,2,1,0:T(8,128)(2,1)}, u32[]{:S(2)}, u32[]{:S(2)}) collective-permute-start(bf16[2,2,192,1152]{3,2,1,0:T(8,128)(2,1)} %dynamic-slice_bitcast_fusion), channel_id=1, source_target_pairs={{0,4},{4,0},{8,12},{12,8},{16,20},{20,16},{24,28},{28,24},{1,5},{5... | collective-permute-start | bytes 5308424 | tf_op jit(solution)/shard_map/ppermute | solution.py:108
  1327.8 39.0 %collective-permute-start.132 = (bf16[2,192,1152]{2,1,0:T(8,128)(2,1)S(1)}, bf16[2,192,1152]{2,1,0:T(8,128)(2,1)S(1)}, u32[]{:S(2)}, u32[]{:S(2)}) collective-permute-start(bf16[2,192,1152]{2,1,0:T(8,128)(2,1)S(1)} %dynamic-slice_bitcast_fusion.8), channel_id=1, source_target_pairs={{0,16},{4,20},{8,24},{12,28},{16,0},{20,4},{24,8},{28,12},{1,17},{... | collective-permute-start | bytes 2654216 | tf_op jit(solution)/shard_map/ppermute | solution.py:108
  1330.6 36.4 %collective-permute-start.136 = (bf16[48,1536]{1,0:T(8,128)(2,1)S(1)}, bf16[48,1536]{1,0:T(8,128)(2,1)S(1)}, u32[]{:S(2)}, u32[]{:S(2)}) collective-permute-start(bf16[48,1536]{1,0:T(8,128)(2,1)S(1)} %dynamic-slice_bitcast_fusion.26), channel_id=1, source_target_pairs={{0,8},{4,12},{8,0},{12,4},{16,24},{20,28},{24,16},{28,20},{1,9},{5... | collective-permute-start | bytes 442376 | tf_op jit(solution)/shard_map/ppermute | solution.py:108
  (333 other events, 5512.0 us)
